TPU v7x, 512 devices: a whole 4x8x8 slice. The times are simulated.
512 devices in a mesh: gx: 16 (over x, y_lo, core), gy: 4 (over y_hi), gz: 8 (over z).
Axes of the slice: x: 4, y: 8 (y_hi: 4, y_lo: 2; y = y_hi * 2 + y_lo), z: 8, core: 2. Of those that a mesh axis runs over, the one named last changes fastest.
Arguments:
- stress_in: float32 [6, 128, 32, 1024], P(None, 'gx', 'gy', 'gz'), may hold values from -6 to 6
- velocity_in: float32 [3, 128, 32, 1024], P(None, 'gx', 'gy', 'gz'), may hold values from -6 to 6
- lame_lambda: float32 [128, 32, 1024], P('gx', 'gy', 'gz'), may hold values from 0.5 to 2
- shear_modulus: float32 [128, 32, 1024], P('gx', 'gy', 'gz'), may hold values from 0.5 to 2
- buoyancy: float32 [128, 32, 1024], P('gx', 'gy', 'gz'), may hold values from 0.5 to 2
- yield_flags: int32 [128, 32, 1024], P('gx', 'gy', 'gz'), may hold values 0 or 1
- panel_cell: int32 [65536], P(('gx', 'gy', 'gz')), may hold values from 0 to 8191, as said below
- panel_normal: float32 [3, 65536], P(None, ('gx', 'gy', 'gz')), may hold values from -4 to 4
- near_block: float32 [65536, 128], P(('gx', 'gy', 'gz')), may hold values from -0.5 to 0.5
- far_rows: float32 [65536, 256], P(('gx', 'gy', 'gz')), may hold values from -0.375 to 0.375
- far_basis: float32 [4096, 65536], P(('gx', 'gy', 'gz')), may hold values from -0.125 to 0.125
- block_ranks: int32 [512, 32], P(('gx', 'gy', 'gz')), may hold values from 2 to 8
Outputs:
- stress_out: float32 [6, 128, 32, 1024], P(None, 'gx', 'gy', 'gz')
- velocity_out: float32 [3, 128, 32, 1024], P(None, 'gx', 'gy', 'gz')
- displacement: float32 [3, 65536], P(None, ('gx', 'gy', 'gz'))
Inputs may be any that keep to these rules, and one draw needn't show every extreme that they name: `panel_cell`: a flat index into the owning device's block of 8 x 8 x 128 zones.
All inputs are finite; a program needn't handle non-finite values. No bound on the sum of `yield_flags` on one device may be relied on, other than what follows from the above.
Results may differ from a plain program's by a relative error of at most 0.000073.
Values sent between devices are 32-bit elements; how exact they have to be, the bound alone decides.
No kernel may reach another device: no remote copies, remote signals or barrier semaphores. Data moves between devices by JAX's collectives and lax.ppermute only.
A program may use at most 64 MiB of HBM per device.

v0:
```python
import jax
import jax.numpy as jnp
from jax import lax
from jax.sharding import PartitionSpec as P

SUB = 2
RANK = 8
CLUST = 32


time_step = 0.1
softening = 0.4


def padded_2(x, sides, width):
    for axis, dim in sides:
        peers, length = (lax.axis_size(axis), x.shape[dim])
        up = [(i, (i + 1) % peers) for i in range(peers - 1)]
        down = [(j, i) for i, j in up]
        last = lax.slice_in_dim(x, length - width, length, axis=dim)
        first = lax.slice_in_dim(x, 0, width, axis=dim)
        before = lax.ppermute(last, axis, up)
        after = lax.ppermute(first, axis, down)
        x = jnp.concatenate([before, x, after], axis=dim)
    return x


def along_first(field):
    return (field[:, 2:, 1:-1, 1:-1] - field[:, :-2, 1:-1, 1:-1]) * 0.5


def along_second(field):
    return (field[:, 1:-1, 2:, 1:-1] - field[:, 1:-1, :-2, 1:-1]) * 0.5


def along_third(field):
    return (field[:, 1:-1, 1:-1, 2:] - field[:, 1:-1, 1:-1, :-2]) * 0.5


def velocity_update(stress, velocity, material):
    accel_x = along_first(stress[0:1]) + along_second(stress[5:6]) + along_third(stress[4:5])
    accel_y = along_first(stress[5:6]) + along_second(stress[1:2]) + along_third(stress[3:4])
    accel_z = along_first(stress[4:5]) + along_second(stress[3:4]) + along_third(stress[2:3])
    acceleration = jnp.concatenate([accel_x, accel_y, accel_z], axis=0)
    return velocity + time_step * material[2:3] * acceleration


def stress_update(velocity, stress, material):
    speed_x = velocity[0:1]
    speed_y = velocity[1:2]
    speed_z = velocity[2:3]
    strain_xx = along_first(speed_x)
    strain_yy = along_second(speed_y)
    strain_zz = along_third(speed_z)
    strain_yz = 0.5 * (along_third(speed_y) + along_second(speed_z))
    strain_xz = 0.5 * (along_third(speed_x) + along_first(speed_z))
    strain_xy = 0.5 * (along_second(speed_x) + along_first(speed_y))
    lame_first = material[0:1]
    shear = material[1:2]
    soften = material[3:4]
    dilation = strain_xx + strain_yy + strain_zz
    isotropic = (lame_first + 2.0 / 3.0 * shear) * dilation
    change_xx = isotropic + soften * (lame_first * dilation + 2.0 * shear * strain_xx - isotropic)
    change_yy = isotropic + soften * (lame_first * dilation + 2.0 * shear * strain_yy - isotropic)
    change_zz = isotropic + soften * (lame_first * dilation + 2.0 * shear * strain_zz - isotropic)
    change_yz = soften * 2.0 * shear * strain_yz
    change_xz = soften * 2.0 * shear * strain_xz
    change_xy = soften * 2.0 * shear * strain_xy
    change = jnp.concatenate(
        [change_xx, change_yy, change_zz, change_yz, change_xz, change_xy], axis=0
    )
    return stress + time_step * change


def tractions_of(picked, normal):
    first = picked[0] * normal[0] + picked[5] * normal[1] + picked[4] * normal[2]
    second = picked[5] * normal[0] + picked[1] * normal[1] + picked[3] * normal[2]
    third = picked[4] * normal[0] + picked[3] * normal[1] + picked[2] * normal[2]
    return jnp.stack([first, second, third], axis=0)


def per_device(
    stress_in,
    velocity_in,
    lame_lambda,
    shear_modulus,
    buoyancy,
    yield_flags,
    panel_cell,
    panel_normal,
    near_block,
    far_rows,
    far_basis,
    block_ranks,
):
    soften = jnp.where(yield_flags == 1, softening, 1.0).astype(jnp.float32)
    material = jnp.stack([lame_lambda, shear_modulus, buoyancy, soften], axis=0)
    flattened = stress_in.reshape(6, -1)
    picked = jnp.take(flattened, panel_cell, axis=1)
    traction = tractions_of(picked, panel_normal)
    everything = lax.all_gather(traction, ("gx", "gy", "gz"), axis=1, tiled=True)
    stress = stress_in
    velocity = velocity_in
    for substep in range(SUB):
        padded = padded_2(stress, (("gx", 1), ("gy", 2), ("gz", 3)), 1)
        velocity = velocity_update(padded, velocity, material)
        padded = padded_2(velocity, (("gx", 1), ("gy", 2), ("gz", 3)), 1)
        stress = stress_update(padded, stress, material)
    panels_all = everything.shape[1]
    cluster_size = panels_all // CLUST
    basis = far_basis.reshape(RANK, CLUST, cluster_size)
    grouped = everything.reshape(3, CLUST, cluster_size)
    projected = jnp.einsum("rcp,kcp->crk", basis, grouped, precision=lax.Precision.HIGHEST)
    rank_mask = (jnp.arange(RANK, dtype=jnp.int32)[None, :] < block_ranks[0][:, None]).astype(
        jnp.float32
    )
    projected = (projected * rank_mask[:, :, None]).reshape(CLUST * RANK, 3)
    far_term = jnp.einsum("pj,jk->kp", far_rows, projected, precision=lax.Precision.HIGHEST)
    near_term = jnp.einsum("pq,kq->kp", near_block, traction, precision=lax.Precision.HIGHEST)
    return (stress, velocity, near_term + far_term)


def solution(mesh):
    placed = (
        P(None, "gx", "gy", "gz"),
        P(None, "gx", "gy", "gz"),
        P("gx", "gy", "gz"),
        P("gx", "gy", "gz"),
        P("gx", "gy", "gz"),
        P("gx", "gy", "gz"),
        P(("gx", "gy", "gz")),
        P(None, ("gx", "gy", "gz")),
        P(("gx", "gy", "gz"), None),
        P(("gx", "gy", "gz"), None),
        P(("gx", "gy", "gz"), None),
        P(("gx", "gy", "gz"), None),
    )
    return jax.shard_map(
        per_device,
        mesh=mesh,
        in_specs=placed,
        out_specs=(
            P(None, "gx", "gy", "gz"),
            P(None, "gx", "gy", "gz"),
            P(None, ("gx", "gy", "gz")),
        ),
        check_vma=False,
    )
```

profile of v0, /device:TPU:1, one launch (start us, length us, event | category | flops | bytes accessed | tf_op | source)
XLA Modules:
  0.0 1374.8 jit_solution(15620191828874151631)
XLA Ops:
  1.6 4.6 collective-permute-start.1
  6.2 5.5 collective-permute-start
  13.5 1.3 collective-permute-start.2
  14.8 4.9 collective-permute-start.3
  20.9 1.4 collective-permute-start.4
  22.4 4.0 collective-permute-start.5
  26.4 8.8 collective-permute-done.4
  36.5 3.6 collective-permute-start.6
  40.1 2.3 collective-permute-start.7
  42.5 2.7 copy.74
  45.2 2.8 gather_fusion
  48.2 1.3 collective-permute-start.8
  49.5 6.1 collective-permute-start.9
  56.6 1.3 collective-permute-start.10
  57.9 4.8 collective-permute-start.11
  62.7 3.8 collective-permute-done.10
  67.9 3.3 collective-permute-start.12
  71.2 3.5 collective-permute-start.13
  75.7 1.3 collective-permute-start.14
  77.0 6.6 collective-permute-start.15
  83.6 1188.0 %all_gather.3 = f32[3,65536]{1,0:T(4,128)S(1)} all-gather(f32[3,128]{1,0:T(4,128)S(1)} %pad_maximum_fusion.75), channel_id=1, replica_groups=mesh['gx'=16,'gy'=4,'gz'=8] {'gx','gy','gz'}, dimensions={1}, use_global_device_ids=true | all-gather | bytes 787968 | tf_op jit(solution)/shard_map/all_gather | solution.py:101
  1273.2 4.0 collective-permute-start.17
  1277.3 4.2 collective-permute-done.16
  1281.5 1.5 collective-permute-done.17
  1283.5 67.0 %collective-permute-start.18 = (f32[3,1,8,128]{3,2,1,0:T(8,128)S(1)}, f32[3,1,8,128]{3,2,1,0:T(8,128)S(1)}, u32[]{:S(2)}, u32[]{:S(2)}) collective-permute-start(f32[3,1,8,128]{3,2,1,0:T(8,128)S(1)} %get-tuple-element.36), channel_id=1, source_target_pairs={{32,0},{64,32},{96,64},{128,96},{160,128},{192,160},{224,192},{256... | collective-permute-start | bytes 36872 | tf_op jit(solution)/shard_map/ppermute | solution.py:23
  1350.5 1.9 collective-permute-start.19
  1352.4 4.3 fusion
  1356.7 1.3 collective-permute-start.20
  1358.0 4.9 collective-permute-start.21
  1364.0 1.3 collective-permute-start.22
  1365.3 4.7 collective-permute-start.23
  1370.8 1.9 collective-permute-done.22
  (98 shorter events, 14.6 us)
Async XLA Ops:
  0.6 1351.8 %copy-start = (f32[8,65536]{1,0:T(8,128)S(1)}, f32[8,65536]{1,0:T(8,128)}, u32[]{:S(2)}) copy-start(f32[8,65536]{1,0:T(8,128)} %param.22) | copy-start | bytes 6291460
  0.6 25.8 %copy-start.11 = (s32[128]{0:T(128)S(1)}, s32[128]{0:T(128)}, u32[]{:S(2)}) copy-start(s32[128]{0:T(128)} %param.18) | copy-start | bytes 1540
  1.6 10.8 collective-permute-start.1
  6.2 7.2 collective-permute-start
  13.5 6.9 collective-permute-start.2
  14.8 5.9 collective-permute-start.3
  20.9 14.2 %collective-permute-start.4 = (f32[6,10,10,1]{3,2,1,0:T(8,128)S(1)}, f32[6,10,10,1]{3,2,1,0:T(8,128)S(1)}, u32[]{:S(2)}, u32[]{:S(2)}) collective-permute-start(f32[6,10,10,1]{3,2,1,0:T(8,128)S(1)} %get-tuple-element.14), channel_id=1, source_target_pairs={{1,0},{2,1},{3,2},{4,3},{5,4},{6,5},{7,6},{9,8},{10,9},{11,10},{12... | collective-permute-start | bytes 7208 | tf_op jit(solution)/shard_map/ppermute | solution.py:23
  22.4 13.7 collective-permute-start.5
  36.5 11.7 collective-permute-start.6
  40.1 8.0 collective-permute-start.7
  42.5 24.9 %copy-start.2 = (f32[8,8,128]{2,1,0:T(8,128)S(1)}, f32[8,8,128]{2,1,0:T(8,128)}, u32[]{:S(2)}) copy-start(f32[8,8,128]{2,1,0:T(8,128)} %param.15) | copy-start | bytes 98308
  42.5 24.9 %copy-start.4 = (f32[8,8,128]{2,1,0:T(8,128)S(1)}, f32[8,8,128]{2,1,0:T(8,128)}, u32[]{:S(2)}) copy-start(f32[8,8,128]{2,1,0:T(8,128)} %param.14) | copy-start | bytes 98308
  42.5 24.9 %copy-start.8 = (s32[8,8,128]{2,1,0:T(8,128)S(1)}, s32[8,8,128]{2,1,0:T(8,128)}, u32[]{:S(2)}) copy-start(s32[8,8,128]{2,1,0:T(8,128)} %param.17) | copy-start | bytes 98308
  48.2 7.4 collective-permute-start.8
  49.5 6.9 collective-permute-start.9
  56.6 9.9 collective-permute-start.10
  57.9 9.5 collective-permute-start.11
  67.9 1209.4 %copy-start.10 = (s32[1,32]{1,0:T(1,128)S(1)}, s32[1,32]{1,0:T(1,128)}, u32[]{:S(2)}) copy-start(s32[1,32]{1,0:T(1,128)} %param.23) | copy-start | bytes 388
  67.9 6.8 collective-permute-start.12
  71.2 4.4 collective-permute-start.13
  75.7 1195.9 %collective-permute-start.14 = (f32[6,10,1,128]{3,2,1,0:T(1,128)S(1)}, f32[6,10,1,128]{3,2,1,0:T(1,128)S(1)}, u32[]{:S(2)}, u32[]{:S(2)}) collective-permute-start(f32[6,10,1,128]{3,2,1,0:T(1,128)S(1)} %get-tuple-element.19), channel_id=1, source_target_pairs={{8,0},{16,8},{24,16},{9,1},{17,9},{25,17},{10,2},{18,10},{26,18},{... | collective-permute-start | bytes 92168 | tf_op jit(solution)/shard_map/ppermute | solution.py:23
  77.0 1194.6 %collective-permute-start.15 = (f32[6,10,1,128]{3,2,1,0:T(1,128)S(1)}, f32[6,10,1,128]{3,2,1,0:T(1,128)S(1)}, u32[]{:S(2)}, u32[]{:S(2)}) collective-permute-start(f32[6,10,1,128]{3,2,1,0:T(1,128)S(1)} %get-tuple-element.18), channel_id=1, source_target_pairs={{0,8},{8,16},{16,24},{1,9},{9,17},{17,25},{2,10},{10,18},{18,26},{... | collective-permute-start | bytes 92168 | tf_op jit(solution)/shard_map/ppermute | solution.py:22
  1271.9 9.6 collective-permute-start.16
  1273.2 9.8 collective-permute-start.17
  1283.4 79.5 %copy-start.7 = (f32[128,128]{1,0:T(8,128)S(1)}, f32[128,128]{1,0:T(8,128)}, u32[]{:S(2)}) copy-start(f32[128,128]{1,0:T(8,128)} %param.20) | copy-start | bytes 196612
  1283.4 90.6 %copy-start.1 = (f32[3,8,8,128]{3,2,1,0:T(8,128)}, f32[3,8,8,128]{3,2,1,0:T(8,128)S(1)}, u32[]{:S(2)}) copy-start(f32[3,8,8,128]{3,2,1,0:T(8,128)S(1)} %fusion.2) | copy-start | bytes 294916
  1283.5 73.2 %collective-permute-start.18 = (f32[3,1,8,128]{3,2,1,0:T(8,128)S(1)}, f32[3,1,8,128]{3,2,1,0:T(8,128)S(1)}, u32[]{:S(2)}, u32[]{:S(2)}) collective-permute-start(f32[3,1,8,128]{3,2,1,0:T(8,128)S(1)} %get-tuple-element.36), channel_id=1, source_target_pairs={{32,0},{64,32},{96,64},{128,96},{160,128},{192,160},{224,192},{256... | collective-permute-start | bytes 36872 | tf_op jit(solution)/shard_map/ppermute | solution.py:23
  1350.5 6.2 collective-permute-start.19
  1356.7 6.5 collective-permute-start.20
  1358.0 5.7 collective-permute-start.21
  1364.0 8.7 collective-permute-start.22
  1365.3 8.3 collective-permute-start.23
  (4 other events, 59.7 us)
where the time goes:
time: 1380 us; the launch traced here: 1370 us
  blocking collectives  1190 us (86%)
  starting transfers between devices  142 us (10%)
  waiting for transfers between devices  25.4 us (2%)
    all_gather x1, blocking collectives, per_device(): lax.all_gather(traction, ('gx', 'gy', 'gz'), axis=1, tiled=True)  1190 us
    ppermute x12, starting transfers between devices, padded_2(): after = lax.ppermute(first, axis, down)  89.9 us
    ppermute x12, starting transfers between devices, padded_2(): before = lax.ppermute(last, axis, up)  52.3 us
  transfers between devices with their start and end apart: 24, of which 12 were waited for; matrix products, arithmetic and copies ran while one was open for 1% of the time, Pallas kernels for 0%

commit v1 on v0

--- a/solution.py
+++ b/solution.py
@@ -6,6 +6,8 @@
 SUB = 2
 RANK = 8
 CLUST = 32
+GX = ("x", "yl", "c")
+ALL = GX + ("gy", "gz")
 
 
 time_step = 0.1
@@ -79,6 +81,24 @@
     return jnp.stack([first, second, third], axis=0)
 
 
+def spread(x, axes):
+    peers = lax.axis_size(axes)
+    return lax.all_to_all(jnp.broadcast_to(x[None], (peers,) + x.shape), axes, 0, 0)
+
+
+def gathered(traction):
+    block = spread(traction, "gz")
+    block = spread(block, ("gy", "yl"))
+    block = spread(block, "x")
+    other = lax.ppermute(block, "c", [(0, 1), (1, 0)])
+    mine = lax.axis_index("c") == 0
+    both = jnp.stack([jnp.where(mine, block, other), jnp.where(mine, other, block)], axis=0)
+    c, x, y, z, k, q = both.shape
+    yl = lax.axis_size("yl")
+    both = both.reshape(c, x, y // yl, yl, z, k, q).transpose(5, 1, 3, 0, 2, 4, 6)
+    return both.reshape(k, CLUST, -1)
+
+
 def per_device(
     stress_in,
     velocity_in,
@@ -98,18 +118,17 @@
     flattened = stress_in.reshape(6, -1)
     picked = jnp.take(flattened, panel_cell, axis=1)
     traction = tractions_of(picked, panel_normal)
-    everything = lax.all_gather(traction, ("gx", "gy", "gz"), axis=1, tiled=True)
+    everything = gathered(traction)
     stress = stress_in
     velocity = velocity_in
     for substep in range(SUB):
-        padded = padded_2(stress, (("gx", 1), ("gy", 2), ("gz", 3)), 1)
+        padded = padded_2(stress, ((GX, 1), ("gy", 2), ("gz", 3)), 1)
         velocity = velocity_update(padded, velocity, material)
-        padded = padded_2(velocity, (("gx", 1), ("gy", 2), ("gz", 3)), 1)
+        padded = padded_2(velocity, ((GX, 1), ("gy", 2), ("gz", 3)), 1)
         stress = stress_update(padded, stress, material)
-    panels_all = everything.shape[1]
-    cluster_size = panels_all // CLUST
+    cluster_size = everything.shape[2]
     basis = far_basis.reshape(RANK, CLUST, cluster_size)
-    grouped = everything.reshape(3, CLUST, cluster_size)
+    grouped = everything
     projected = jnp.einsum("rcp,kcp->crk", basis, grouped, precision=lax.Precision.HIGHEST)
     rank_mask = (jnp.arange(RANK, dtype=jnp.int32)[None, :] < block_ranks[0][:, None]).astype(
         jnp.float32
@@ -121,28 +140,29 @@
 
 
 def solution(mesh):
-    placed = (
-        P(None, "gx", "gy", "gz"),
-        P(None, "gx", "gy", "gz"),
-        P("gx", "gy", "gz"),
-        P("gx", "gy", "gz"),
-        P("gx", "gy", "gz"),
-        P("gx", "gy", "gz"),
-        P(("gx", "gy", "gz")),
-        P(None, ("gx", "gy", "gz")),
-        P(("gx", "gy", "gz"), None),
-        P(("gx", "gy", "gz"), None),
-        P(("gx", "gy", "gz"), None),
-        P(("gx", "gy", "gz"), None),
+    shape = dict(mesh.shape)
+    fine = jax.sharding.Mesh(
+        mesh.devices.reshape(shape["gx"] // 4, 2, 2, shape["gy"], shape["gz"]), ALL
     )
+    zones = P(GX, "gy", "gz")
+    fields = P(None, GX, "gy", "gz")
     return jax.shard_map(
         per_device,
-        mesh=mesh,
-        in_specs=placed,
-        out_specs=(
-            P(None, "gx", "gy", "gz"),
-            P(None, "gx", "gy", "gz"),
-            P(None, ("gx", "gy", "gz")),
+        mesh=fine,
+        in_specs=(
+            fields,
+            fields,
+            zones,
+            zones,
+            zones,
+            zones,
+            P(ALL),
+            P(None, ALL),
+            P(ALL, None),
+            P(ALL, None),
+            P(ALL, None),
+            P(ALL, None),
         ),
+        out_specs=(fields, fields, P(None, ALL)),
         check_vma=False,
     )

time: 1380 us -> 184 us (0.13)
  blocking collectives: 1190 us -> 0 us
  starting transfers between devices: 142 us -> 116 us
    all_gather x1 -> x0, blocking collectives: 1190 us -> none  [per_device(): lax.all_gather(traction, ('gx', 'gy', 'gz'), axis=1, tiled=True)]
    ppermute x12, starting transfers between devices: 89.9 us -> 24.8 us  [padded_2(): after = lax.ppermute(first, axis, down)]
    all_to_all x0 -> x3, starting transfers between devices: none -> 28.3 us  [spread(): lax.all_to_all(jnp.broadcast_to(x[None], (peers,) + x.shape), axes, 0, 0)]
  transfers between devices with their start and end apart: 24 -> 28, of which waited for: 12 -> 13; matrix products, arithmetic and copies ran while one was open for 1% -> 8% of each run, Pallas kernels for 0% -> 0%
where the time goes in v1:
time: 184 us; the launch traced here: 183 us
  starting transfers between devices  116 us (63%)
  waiting for transfers between devices  39 us (21%)
  local copies, waits for them, and re-layouts  13.4 us (7%)
  other arithmetic  7.55 us (4%)
  matrix products  5.65 us (3%)
    ppermute x12, starting transfers between devices, padded_2(): before = lax.ppermute(last, axis, up)  57.4 us
    all_to_all x3, starting transfers between devices, spread(): lax.all_to_all(jnp.broadcast_to(x[None], (peers,) + x.shape), axes, 0, 0)  28.3 us
    ppermute x12, starting transfers between devices, padded_2(): after = lax.ppermute(first, axis, down)  24.8 us
    ppermute x12, waiting for transfers between devices, padded_2(): after = lax.ppermute(first, axis, down)  21 us
    all_to_all x3, waiting for transfers between devices, spread(): lax.all_to_all(jnp.broadcast_to(x[None], (peers,) + x.shape), axes, 0, 0)  10.2 us
    ppermute x12, waiting for transfers between devices, padded_2(): before = lax.ppermute(last, axis, up)  7.84 us
    ppermute x1, starting transfers between devices, gathered(): other = lax.ppermute(block, 'c', [(0, 1), (1, 0)])  5.87 us
    dot_general x1, matrix products, per_device(): jnp.einsum('rcp,kcp->crk', basis, grouped, precision=lax.Precision.HIGHEST)  4.68 us
  transfers between devices with their start and end apart: 28, of which 13 were waited for; matrix products, arithmetic and copies ran while one was open for 8% of the time, Pallas kernels for 0%

profile of v1, /device:TPU:1, one launch (start us, length us, event | category | flops | bytes accessed | tf_op | source)
XLA Modules:
  0.0 183.4 jit_solution(15968039897015039586)
XLA Ops:
  1.6 4.6 %collective-permute-start.1 = (f32[6,1,8,128]{3,2,1,0:T(8,128)S(1)}, f32[6,1,8,128]{3,2,1,0:T(8,128)S(1)}, u32[]{:S(2)}, u32[]{:S(2)}) collective-permute-start(f32[6,1,8,128]{3,2,1,0:T(8,128)S(1)} %get-tuple-element.32), channel_id=1, source_target_pairs={{0,32},{32,64},{64,96},{96,128},{128,160},{160,192},{192,224},{224... | collective-permute-start | bytes 73736 | tf_op jit(solution)/shard_map/ppermute | solution.py:24
  6.2 5.5 %collective-permute-start = (f32[6,1,8,128]{3,2,1,0:T(8,128)S(1)}, f32[6,1,8,128]{3,2,1,0:T(8,128)S(1)}, u32[]{:S(2)}, u32[]{:S(2)}) collective-permute-start(f32[6,1,8,128]{3,2,1,0:T(8,128)S(1)} %get-tuple-element.31), channel_id=1, source_target_pairs={{32,0},{64,32},{96,64},{128,96},{160,128},{192,160},{224,192},{256... | collective-permute-start | bytes 73736 | tf_op jit(solution)/shard_map/ppermute | solution.py:25
  14.0 4.9 %collective-permute-start.3 = (f32[6,10,1,128]{3,2,1,0:T(1,128)S(1)}, f32[6,10,1,128]{3,2,1,0:T(1,128)S(1)}, u32[]{:S(2)}, u32[]{:S(2)}) collective-permute-start(f32[6,10,1,128]{3,2,1,0:T(1,128)S(1)} %get-tuple-element.24), channel_id=1, source_target_pairs={{0,8},{8,16},{16,24},{1,9},{9,17},{17,25},{2,10},{10,18},{18,26},{... | collective-permute-start | bytes 92168 | tf_op jit(solution)/shard_map/ppermute | solution.py:24
  21.5 4.0 %collective-permute-start.5 = (f32[6,10,10,1]{3,2,1,0:T(8,128)S(1)}, f32[6,10,10,1]{3,2,1,0:T(8,128)S(1)}, u32[]{:S(2)}, u32[]{:S(2)}) collective-permute-start(f32[6,10,10,1]{3,2,1,0:T(8,128)S(1)} %get-tuple-element.17), channel_id=1, source_target_pairs={{0,1},{1,2},{2,3},{3,4},{4,5},{5,6},{6,7},{8,9},{9,10},{10,11},{11... | collective-permute-start | bytes 7208 | tf_op jit(solution)/shard_map/ppermute | solution.py:24
  25.5 7.9 %collective-permute-done.4 = f32[6,10,10,1]{3,2,1,0:T(8,128)S(1)} collective-permute-done((f32[6,10,10,1]{3,2,1,0:T(8,128)S(1)}, f32[6,10,10,1]{3,2,1,0:T(8,128)S(1)}, u32[]{:S(2)}, u32[]{:S(2)}) %collective-permute-start.4) | collective-permute-done | bytes 2432 | tf_op jit(solution)/shard_map/ppermute | solution.py:25
  34.9 4.4 %collective-permute-start.6 = (f32[3,1,8,128]{3,2,1,0:T(8,128)S(1)}, f32[3,1,8,128]{3,2,1,0:T(8,128)S(1)}, u32[]{:S(2)}, u32[]{:S(2)}) collective-permute-start(f32[3,1,8,128]{3,2,1,0:T(8,128)S(1)} %get-tuple-element.40), channel_id=1, source_target_pairs={{32,0},{64,32},{96,64},{128,96},{160,128},{192,160},{224,192},{256... | collective-permute-start | bytes 36872 | tf_op jit(solution)/shard_map/ppermute | solution.py:25
  39.3 2.5 %collective-permute-start.7 = (f32[3,1,8,128]{3,2,1,0:T(8,128)S(1)}, f32[3,1,8,128]{3,2,1,0:T(8,128)S(1)}, u32[]{:S(2)}, u32[]{:S(2)}) collective-permute-start(f32[3,1,8,128]{3,2,1,0:T(8,128)S(1)} %get-tuple-element.39), channel_id=1, source_target_pairs={{0,32},{32,64},{64,96},{96,128},{128,160},{160,192},{192,224},{224... | collective-permute-start | bytes 36872 | tf_op jit(solution)/shard_map/ppermute | solution.py:24
  42.6 1.3 collective-permute-start.8
  43.9 6.1 %collective-permute-start.9 = (f32[3,10,1,128]{3,2,1,0:T(1,128)S(1)}, f32[3,10,1,128]{3,2,1,0:T(1,128)S(1)}, u32[]{:S(2)}, u32[]{:S(2)}) collective-permute-start(f32[3,10,1,128]{3,2,1,0:T(1,128)S(1)} %get-tuple-element.36), channel_id=1, source_target_pairs={{0,8},{8,16},{16,24},{1,9},{9,17},{17,25},{2,10},{10,18},{18,26},{... | collective-permute-start | bytes 46088 | tf_op jit(solution)/shard_map/ppermute | solution.py:24
  52.3 4.7 %collective-permute-start.11 = (f32[3,10,10,1]{3,2,1,0:T(8,128)S(1)}, f32[3,10,10,1]{3,2,1,0:T(8,128)S(1)}, u32[]{:S(2)}, u32[]{:S(2)}) collective-permute-start(f32[3,10,10,1]{3,2,1,0:T(8,128)S(1)} %get-tuple-element.23), channel_id=1, source_target_pairs={{0,1},{1,2},{2,3},{3,4},{4,5},{5,6},{6,7},{8,9},{9,10},{10,11},{11... | collective-permute-start | bytes 3608 | tf_op jit(solution)/shard_map/ppermute | solution.py:24
  57.1 4.3 %collective-permute-done.10 = f32[3,10,10,1]{3,2,1,0:T(8,128)S(1)} collective-permute-done((f32[3,10,10,1]{3,2,1,0:T(8,128)S(1)}, f32[3,10,10,1]{3,2,1,0:T(8,128)S(1)}, u32[]{:S(2)}, u32[]{:S(2)}) %collective-permute-start.10) | collective-permute-done | bytes 1232 | tf_op jit(solution)/shard_map/ppermute | solution.py:25
  63.0 2.7 %collective-permute-start.12 = (f32[6,1,8,128]{3,2,1,0:T(8,128)S(1)}, f32[6,1,8,128]{3,2,1,0:T(8,128)S(1)}, u32[]{:S(2)}, u32[]{:S(2)}) collective-permute-start(f32[6,1,8,128]{3,2,1,0:T(8,128)S(1)} %get-tuple-element.27), channel_id=1, source_target_pairs={{32,0},{64,32},{96,64},{128,96},{160,128},{192,160},{224,192},{256... | collective-permute-start | bytes 73736 | tf_op jit(solution)/shard_map/ppermute | solution.py:25
  65.7 4.3 %collective-permute-start.13 = (f32[6,1,8,128]{3,2,1,0:T(8,128)S(1)}, f32[6,1,8,128]{3,2,1,0:T(8,128)S(1)}, u32[]{:S(2)}, u32[]{:S(2)}) collective-permute-start(f32[6,1,8,128]{3,2,1,0:T(8,128)S(1)} %get-tuple-element.26), channel_id=1, source_target_pairs={{0,32},{32,64},{64,96},{96,128},{128,160},{160,192},{192,224},{224... | collective-permute-start | bytes 73736 | tf_op jit(solution)/shard_map/ppermute | solution.py:24
  70.0 2.7 %copy.100 = f32[6,8,8,128]{0,3,2,1:T(8,128)} copy(f32[6,8,8,128]{3,2,1,0:T(8,128)S(1)} %copy-done.3) | data formatting | bytes 393216 | tf_op args[0]
  72.8 2.8 %gather_fusion = f32[128,6]{1,0:T(8,128)S(1)} fusion(f32[6,8192]{0,1:T(8,128)} %bitcast.145, s32[1024]{0:T(1024)S(1)} %pad_clamp_fusion), kind=kCustom, calls=%fused_computation | custom fusion | bytes 6656 | tf_op jit(solution)/shard_map/jit(_take)/gather | solution.py:119
  75.7 1.3 collective-permute-start.14
  77.0 6.7 %collective-permute-start.15 = (f32[6,10,1,128]{3,2,1,0:T(1,128)S(1)}, f32[6,10,1,128]{3,2,1,0:T(1,128)S(1)}, u32[]{:S(2)}, u32[]{:S(2)}) collective-permute-start(f32[6,10,1,128]{3,2,1,0:T(1,128)S(1)} %get-tuple-element.20), channel_id=1, source_target_pairs={{0,8},{8,16},{16,24},{1,9},{9,17},{17,25},{2,10},{10,18},{18,26},{... | collective-permute-start | bytes 92168 | tf_op jit(solution)/shard_map/ppermute | solution.py:24
  86.4 4.8 %collective-permute-start.17 = (f32[6,10,10,1]{3,2,1,0:T(8,128)S(1)}, f32[6,10,10,1]{3,2,1,0:T(8,128)S(1)}, u32[]{:S(2)}, u32[]{:S(2)}) collective-permute-start(f32[6,10,10,1]{3,2,1,0:T(8,128)S(1)} %get-tuple-element.15), channel_id=1, source_target_pairs={{0,1},{1,2},{2,3},{3,4},{4,5},{5,6},{6,7},{8,9},{9,10},{10,11},{11... | collective-permute-start | bytes 7208 | tf_op jit(solution)/shard_map/ppermute | solution.py:24
  91.2 8.6 %collective-permute-done.16 = f32[6,10,10,1]{3,2,1,0:T(8,128)S(1)} collective-permute-done((f32[6,10,10,1]{3,2,1,0:T(8,128)S(1)}, f32[6,10,10,1]{3,2,1,0:T(8,128)S(1)}, u32[]{:S(2)}, u32[]{:S(2)}) %collective-permute-start.16) | collective-permute-done | bytes 2432 | tf_op jit(solution)/shard_map/ppermute | solution.py:25
  99.8 1.8 collective-permute-done.17
  102.0 1.9 %collective-permute-start.18 = (f32[3,1,8,128]{3,2,1,0:T(8,128)S(1)}, f32[3,1,8,128]{3,2,1,0:T(8,128)S(1)}, u32[]{:S(2)}, u32[]{:S(2)}) collective-permute-start(f32[3,1,8,128]{3,2,1,0:T(8,128)S(1)} %get-tuple-element.38), channel_id=1, source_target_pairs={{32,0},{64,32},{96,64},{128,96},{160,128},{192,160},{224,192},{256... | collective-permute-start | bytes 36872 | tf_op jit(solution)/shard_map/ppermute | solution.py:25
  103.9 4.6 %collective-permute-start.19 = (f32[3,1,8,128]{3,2,1,0:T(8,128)S(1)}, f32[3,1,8,128]{3,2,1,0:T(8,128)S(1)}, u32[]{:S(2)}, u32[]{:S(2)}) collective-permute-start(f32[3,1,8,128]{3,2,1,0:T(8,128)S(1)} %get-tuple-element.37), channel_id=1, source_target_pairs={{0,32},{32,64},{64,96},{96,128},{128,160},{160,192},{192,224},{224... | collective-permute-start | bytes 36872 | tf_op jit(solution)/shard_map/ppermute | solution.py:24
  109.2 13.7 %all-to-all-start = ((f32[8,3,128]{2,1,0:T(4,128)}), f32[8,3,128]{2,1,0:T(4,128)S(1)}, u32[]{:S(2)}, u32[]{:S(2)}) async-start(f32[8,3,128]{2,1,0:T(4,128)} %broadcast_in_dim.45), calls=%async_computation | async-start | bytes 32768 | tf_op jit(solution)/shard_map/all_to_all | solution.py:86
  124.3 6.1 %collective-permute-start.21 = (f32[3,10,1,128]{3,2,1,0:T(1,128)S(1)}, f32[3,10,1,128]{3,2,1,0:T(1,128)S(1)}, u32[]{:S(2)}, u32[]{:S(2)}) collective-permute-start(f32[3,10,1,128]{3,2,1,0:T(1,128)S(1)} %get-tuple-element.34), channel_id=1, source_target_pairs={{0,8},{8,16},{16,24},{1,9},{9,17},{17,25},{2,10},{10,18},{18,26},{... | collective-permute-start | bytes 46088 | tf_op jit(solution)/shard_map/ppermute | solution.py:24
  133.4 4.0 %collective-permute-start.23 = (f32[3,10,10,1]{3,2,1,0:T(8,128)S(1)}, f32[3,10,10,1]{3,2,1,0:T(8,128)S(1)}, u32[]{:S(2)}, u32[]{:S(2)}) collective-permute-start(f32[3,10,10,1]{3,2,1,0:T(8,128)S(1)} %get-tuple-element.19), channel_id=1, source_target_pairs={{0,1},{1,2},{2,3},{3,4},{4,5},{5,6},{6,7},{8,9},{9,10},{10,11},{11... | collective-permute-start | bytes 3608 | tf_op jit(solution)/shard_map/ppermute | solution.py:24
  138.1 10.2 %all-to-all-start.1 = ((f32[8,8,3,128]{3,1,2,0:T(8,128)}), f32[8,8,3,128]{3,1,2,0:T(8,128)S(1)}, u32[]{:S(2)}, u32[]{:S(2)}) async-start(f32[8,8,3,128]{3,1,2,0:T(8,128)} %broadcast_in_dim.46), calls=%async_computation.1 | async-start | bytes 196608 | tf_op jit(solution)/shard_map/all_to_all | solution.py:86
  150.3 5.4 %all-to-all-done.1 = f32[8,8,3,128]{3,1,2,0:T(8,128)S(1)} async-done(((f32[8,8,3,128]{3,1,2,0:T(8,128)}), f32[8,8,3,128]{3,1,2,0:T(8,128)S(1)}, u32[]{:S(2)}, u32[]{:S(2)}) %all-to-all-start.1) | async-done | bytes 98336 | tf_op jit(solution)/shard_map/all_to_all | solution.py:86
  156.5 4.4 %all-to-all-start.2 = ((f32[4,8,8,3,128]{4,2,3,1,0:T(8,128)}), f32[4,8,8,3,128]{4,2,3,1,0:T(8,128)S(1)}, u32[]{:S(2)}, u32[]{:S(2)}) async-start(f32[4,8,8,3,128]{4,2,3,1,0:T(8,128)} %broadcast_in_dim.47), calls=%async_computation.2 | async-start | bytes 786432 | tf_op jit(solution)/shard_map/all_to_all | solution.py:86
  162.3 4.8 %all-to-all-done.2 = f32[4,8,8,3,128]{4,2,3,1,0:T(8,128)S(1)} async-done(((f32[4,8,8,3,128]{4,2,3,1,0:T(8,128)}), f32[4,8,8,3,128]{4,2,3,1,0:T(8,128)S(1)}, u32[]{:S(2)}, u32[]{:S(2)}) %all-to-all-start.2) | async-done | bytes 393248 | tf_op jit(solution)/shard_map/all_to_all | solution.py:86
  167.1 5.9 %collective-permute-start.24 = (f32[4,8,8,3,128]{4,2,3,1,0:T(8,128)S(1)}, f32[4,8,8,3,128]{4,2,3,1,0:T(8,128)S(1)}, u32[]{:S(2)}, u32[]{:S(2)}) collective-permute-start(f32[4,8,8,3,128]{4,2,3,1,0:T(8,128)S(1)} %all-to-all-done.2), channel_id=1, source_target_pairs={{0,32},{32,0},{1,33},{33,1},{2,34},{34,2},{3,35},{35,3},{4,36},{36... | collective-permute-start | bytes 1179656 | tf_op jit(solution)/shard_map/ppermute | solution.py:93
  173.7 1.6 multiply_add_fusion
  177.8 4.7 %fusion = f32[32,8,3]{1,2,0:T(4,128)S(1)} fusion(f32[8,32,2048]{2,0,1:T(8,128)S(1)} %bitcast.144, f32[3,32,2048]{2,1,0:T(8,128)S(1)} %reshape.64, f32[32,8]{1,0:T(8,128)S(1)} %fusion.83), kind=kOutput, calls=%fused_computation.2 | convolution fusion | flops 18875136 | bytes 2887680 | tf_op jit(solution)/shard_map/rcp,kcp->crk/dot_general | solution.py:132
  (115 shorter events, 28.6 us)
Async XLA Ops:
  0.6 177.1 %copy-start = (f32[8,65536]{1,0:T(8,128)S(1)}, f32[8,65536]{1,0:T(8,128)}, u32[]{:S(2)}) copy-start(f32[8,65536]{1,0:T(8,128)} %param.22) | copy-start | bytes 6291460
  1.6 10.1 %collective-permute-start.1 = (f32[6,1,8,128]{3,2,1,0:T(8,128)S(1)}, f32[6,1,8,128]{3,2,1,0:T(8,128)S(1)}, u32[]{:S(2)}, u32[]{:S(2)}) collective-permute-start(f32[6,1,8,128]{3,2,1,0:T(8,128)S(1)} %get-tuple-element.32), channel_id=1, source_target_pairs={{0,32},{32,64},{64,96},{96,128},{128,160},{160,192},{192,224},{224... | collective-permute-start | bytes 73736 | tf_op jit(solution)/shard_map/ppermute | solution.py:24
  6.2 6.5 %collective-permute-start = (f32[6,1,8,128]{3,2,1,0:T(8,128)S(1)}, f32[6,1,8,128]{3,2,1,0:T(8,128)S(1)}, u32[]{:S(2)}, u32[]{:S(2)}) collective-permute-start(f32[6,1,8,128]{3,2,1,0:T(8,128)S(1)} %get-tuple-element.31), channel_id=1, source_target_pairs={{32,0},{64,32},{96,64},{128,96},{160,128},{192,160},{224,192},{256... | collective-permute-start | bytes 73736 | tf_op jit(solution)/shard_map/ppermute | solution.py:25
  12.7 6.2 %collective-permute-start.2 = (f32[6,10,1,128]{3,2,1,0:T(1,128)S(1)}, f32[6,10,1,128]{3,2,1,0:T(1,128)S(1)}, u32[]{:S(2)}, u32[]{:S(2)}) collective-permute-start(f32[6,10,1,128]{3,2,1,0:T(1,128)S(1)} %get-tuple-element.25), channel_id=1, source_target_pairs={{8,0},{16,8},{24,16},{9,1},{17,9},{25,17},{10,2},{18,10},{26,18},{... | collective-permute-start | bytes 92168 | tf_op jit(solution)/shard_map/ppermute | solution.py:25
  14.0 5.9 %collective-permute-start.3 = (f32[6,10,1,128]{3,2,1,0:T(1,128)S(1)}, f32[6,10,1,128]{3,2,1,0:T(1,128)S(1)}, u32[]{:S(2)}, u32[]{:S(2)}) collective-permute-start(f32[6,10,1,128]{3,2,1,0:T(1,128)S(1)} %get-tuple-element.24), channel_id=1, source_target_pairs={{0,8},{8,16},{16,24},{1,9},{9,17},{17,25},{2,10},{10,18},{18,26},{... | collective-permute-start | bytes 92168 | tf_op jit(solution)/shard_map/ppermute | solution.py:24
  20.2 13.3 %collective-permute-start.4 = (f32[6,10,10,1]{3,2,1,0:T(8,128)S(1)}, f32[6,10,10,1]{3,2,1,0:T(8,128)S(1)}, u32[]{:S(2)}, u32[]{:S(2)}) collective-permute-start(f32[6,10,10,1]{3,2,1,0:T(8,128)S(1)} %get-tuple-element.16), channel_id=1, source_target_pairs={{1,0},{2,1},{3,2},{4,3},{5,4},{6,5},{7,6},{9,8},{10,9},{11,10},{12... | collective-permute-start | bytes 7208 | tf_op jit(solution)/shard_map/ppermute | solution.py:25
  21.5 12.9 %collective-permute-start.5 = (f32[6,10,10,1]{3,2,1,0:T(8,128)S(1)}, f32[6,10,10,1]{3,2,1,0:T(8,128)S(1)}, u32[]{:S(2)}, u32[]{:S(2)}) collective-permute-start(f32[6,10,10,1]{3,2,1,0:T(8,128)S(1)} %get-tuple-element.17), channel_id=1, source_target_pairs={{0,1},{1,2},{2,3},{3,4},{4,5},{5,6},{6,7},{8,9},{9,10},{10,11},{11... | collective-permute-start | bytes 7208 | tf_op jit(solution)/shard_map/ppermute | solution.py:24
  34.9 7.0 %collective-permute-start.6 = (f32[3,1,8,128]{3,2,1,0:T(8,128)S(1)}, f32[3,1,8,128]{3,2,1,0:T(8,128)S(1)}, u32[]{:S(2)}, u32[]{:S(2)}) collective-permute-start(f32[3,1,8,128]{3,2,1,0:T(8,128)S(1)} %get-tuple-element.40), channel_id=1, source_target_pairs={{32,0},{64,32},{96,64},{128,96},{160,128},{192,160},{224,192},{256... | collective-permute-start | bytes 36872 | tf_op jit(solution)/shard_map/ppermute | solution.py:25
  39.3 3.3 %collective-permute-start.7 = (f32[3,1,8,128]{3,2,1,0:T(8,128)S(1)}, f32[3,1,8,128]{3,2,1,0:T(8,128)S(1)}, u32[]{:S(2)}, u32[]{:S(2)}) collective-permute-start(f32[3,1,8,128]{3,2,1,0:T(8,128)S(1)} %get-tuple-element.39), channel_id=1, source_target_pairs={{0,32},{32,64},{64,96},{96,128},{128,160},{160,192},{192,224},{224... | collective-permute-start | bytes 36872 | tf_op jit(solution)/shard_map/ppermute | solution.py:24
  42.6 7.4 %collective-permute-start.8 = (f32[3,10,1,128]{3,2,1,0:T(1,128)S(1)}, f32[3,10,1,128]{3,2,1,0:T(1,128)S(1)}, u32[]{:S(2)}, u32[]{:S(2)}) collective-permute-start(f32[3,10,1,128]{3,2,1,0:T(1,128)S(1)} %get-tuple-element.35), channel_id=1, source_target_pairs={{8,0},{16,8},{24,16},{9,1},{17,9},{25,17},{10,2},{18,10},{26,18},{... | collective-permute-start | bytes 46088 | tf_op jit(solution)/shard_map/ppermute | solution.py:25
  43.9 6.9 %collective-permute-start.9 = (f32[3,10,1,128]{3,2,1,0:T(1,128)S(1)}, f32[3,10,1,128]{3,2,1,0:T(1,128)S(1)}, u32[]{:S(2)}, u32[]{:S(2)}) collective-permute-start(f32[3,10,1,128]{3,2,1,0:T(1,128)S(1)} %get-tuple-element.36), channel_id=1, source_target_pairs={{0,8},{8,16},{16,24},{1,9},{9,17},{17,25},{2,10},{10,18},{18,26},{... | collective-permute-start | bytes 46088 | tf_op jit(solution)/shard_map/ppermute | solution.py:24
  51.0 10.4 %collective-permute-start.10 = (f32[3,10,10,1]{3,2,1,0:T(8,128)S(1)}, f32[3,10,10,1]{3,2,1,0:T(8,128)S(1)}, u32[]{:S(2)}, u32[]{:S(2)}) collective-permute-start(f32[3,10,10,1]{3,2,1,0:T(8,128)S(1)} %get-tuple-element.22), channel_id=1, source_target_pairs={{1,0},{2,1},{3,2},{4,3},{5,4},{6,5},{7,6},{9,8},{10,9},{11,10},{12... | collective-permute-start | bytes 3608 | tf_op jit(solution)/shard_map/ppermute | solution.py:25
  52.3 10.1 %collective-permute-start.11 = (f32[3,10,10,1]{3,2,1,0:T(8,128)S(1)}, f32[3,10,10,1]{3,2,1,0:T(8,128)S(1)}, u32[]{:S(2)}, u32[]{:S(2)}) collective-permute-start(f32[3,10,10,1]{3,2,1,0:T(8,128)S(1)} %get-tuple-element.23), channel_id=1, source_target_pairs={{0,1},{1,2},{2,3},{3,4},{4,5},{5,6},{6,7},{8,9},{9,10},{10,11},{11... | collective-permute-start | bytes 3608 | tf_op jit(solution)/shard_map/ppermute | solution.py:24
  63.0 12.7 %collective-permute-start.12 = (f32[6,1,8,128]{3,2,1,0:T(8,128)S(1)}, f32[6,1,8,128]{3,2,1,0:T(8,128)S(1)}, u32[]{:S(2)}, u32[]{:S(2)}) collective-permute-start(f32[6,1,8,128]{3,2,1,0:T(8,128)S(1)} %get-tuple-element.27), channel_id=1, source_target_pairs={{32,0},{64,32},{96,64},{128,96},{160,128},{192,160},{224,192},{256... | collective-permute-start | bytes 73736 | tf_op jit(solution)/shard_map/ppermute | solution.py:25
  65.7 10.0 %collective-permute-start.13 = (f32[6,1,8,128]{3,2,1,0:T(8,128)S(1)}, f32[6,1,8,128]{3,2,1,0:T(8,128)S(1)}, u32[]{:S(2)}, u32[]{:S(2)}) collective-permute-start(f32[6,1,8,128]{3,2,1,0:T(8,128)S(1)} %get-tuple-element.26), channel_id=1, source_target_pairs={{0,32},{32,64},{64,96},{96,128},{128,160},{160,192},{192,224},{224... | collective-permute-start | bytes 73736 | tf_op jit(solution)/shard_map/ppermute | solution.py:24
  75.7 8.1 %collective-permute-start.14 = (f32[6,10,1,128]{3,2,1,0:T(1,128)S(1)}, f32[6,10,1,128]{3,2,1,0:T(1,128)S(1)}, u32[]{:S(2)}, u32[]{:S(2)}) collective-permute-start(f32[6,10,1,128]{3,2,1,0:T(1,128)S(1)} %get-tuple-element.21), channel_id=1, source_target_pairs={{8,0},{16,8},{24,16},{9,1},{17,9},{25,17},{10,2},{18,10},{26,18},{... | collective-permute-start | bytes 92168 | tf_op jit(solution)/shard_map/ppermute | solution.py:25
  77.0 7.7 %collective-permute-start.15 = (f32[6,10,1,128]{3,2,1,0:T(1,128)S(1)}, f32[6,10,1,128]{3,2,1,0:T(1,128)S(1)}, u32[]{:S(2)}, u32[]{:S(2)}) collective-permute-start(f32[6,10,1,128]{3,2,1,0:T(1,128)S(1)} %get-tuple-element.20), channel_id=1, source_target_pairs={{0,8},{8,16},{16,24},{1,9},{9,17},{17,25},{2,10},{10,18},{18,26},{... | collective-permute-start | bytes 92168 | tf_op jit(solution)/shard_map/ppermute | solution.py:24
  85.1 14.8 %collective-permute-start.16 = (f32[6,10,10,1]{3,2,1,0:T(8,128)S(1)}, f32[6,10,10,1]{3,2,1,0:T(8,128)S(1)}, u32[]{:S(2)}, u32[]{:S(2)}) collective-permute-start(f32[6,10,10,1]{3,2,1,0:T(8,128)S(1)} %get-tuple-element.14), channel_id=1, source_target_pairs={{1,0},{2,1},{3,2},{4,3},{5,4},{6,5},{7,6},{9,8},{10,9},{11,10},{12... | collective-permute-start | bytes 7208 | tf_op jit(solution)/shard_map/ppermute | solution.py:25
  86.4 15.2 %collective-permute-start.17 = (f32[6,10,10,1]{3,2,1,0:T(8,128)S(1)}, f32[6,10,10,1]{3,2,1,0:T(8,128)S(1)}, u32[]{:S(2)}, u32[]{:S(2)}) collective-permute-start(f32[6,10,10,1]{3,2,1,0:T(8,128)S(1)} %get-tuple-element.15), channel_id=1, source_target_pairs={{0,1},{1,2},{2,3},{3,4},{4,5},{5,6},{6,7},{8,9},{9,10},{10,11},{11... | collective-permute-start | bytes 7208 | tf_op jit(solution)/shard_map/ppermute | solution.py:24
  91.2 39.2 %copy-start.7 = (f32[128,128]{1,0:T(8,128)S(1)}, f32[128,128]{1,0:T(8,128)}, u32[]{:S(2)}) copy-start(f32[128,128]{1,0:T(8,128)} %param.20) | copy-start | bytes 196612
  101.7 35.7 %copy-start.11 = (s32[1,32]{1,0:T(1,128)S(1)}, s32[1,32]{1,0:T(1,128)}, u32[]{:S(2)}) copy-start(s32[1,32]{1,0:T(1,128)} %param.23) | copy-start | bytes 388
  102.0 71.0 %copy-start.1 = (f32[3,8,8,128]{3,2,1,0:T(8,128)}, f32[3,8,8,128]{3,2,1,0:T(8,128)S(1)}, u32[]{:S(2)}) copy-start(f32[3,8,8,128]{3,2,1,0:T(8,128)S(1)} %fusion.3) | copy-start | bytes 294916
  102.0 20.9 %collective-permute-start.18 = (f32[3,1,8,128]{3,2,1,0:T(8,128)S(1)}, f32[3,1,8,128]{3,2,1,0:T(8,128)S(1)}, u32[]{:S(2)}, u32[]{:S(2)}) collective-permute-start(f32[3,1,8,128]{3,2,1,0:T(8,128)S(1)} %get-tuple-element.38), channel_id=1, source_target_pairs={{32,0},{64,32},{96,64},{128,96},{160,128},{192,160},{224,192},{256... | collective-permute-start | bytes 36872 | tf_op jit(solution)/shard_map/ppermute | solution.py:25
  103.9 19.0 %collective-permute-start.19 = (f32[3,1,8,128]{3,2,1,0:T(8,128)S(1)}, f32[3,1,8,128]{3,2,1,0:T(8,128)S(1)}, u32[]{:S(2)}, u32[]{:S(2)}) collective-permute-start(f32[3,1,8,128]{3,2,1,0:T(8,128)S(1)} %get-tuple-element.37), channel_id=1, source_target_pairs={{0,32},{32,64},{64,96},{96,128},{128,160},{160,192},{192,224},{224... | collective-permute-start | bytes 36872 | tf_op jit(solution)/shard_map/ppermute | solution.py:24
  109.2 28.2 %all-to-all-start = ((f32[8,3,128]{2,1,0:T(4,128)}), f32[8,3,128]{2,1,0:T(4,128)S(1)}, u32[]{:S(2)}, u32[]{:S(2)}) async-start(f32[8,3,128]{2,1,0:T(4,128)} %broadcast_in_dim.45), calls=%async_computation | async-start | bytes 32768 | tf_op jit(solution)/shard_map/all_to_all | solution.py:86
  123.0 7.6 %collective-permute-start.20 = (f32[3,10,1,128]{3,2,1,0:T(1,128)S(1)}, f32[3,10,1,128]{3,2,1,0:T(1,128)S(1)}, u32[]{:S(2)}, u32[]{:S(2)}) collective-permute-start(f32[3,10,1,128]{3,2,1,0:T(1,128)S(1)} %get-tuple-element.33), channel_id=1, source_target_pairs={{8,0},{16,8},{24,16},{9,1},{17,9},{25,17},{10,2},{18,10},{26,18},{... | collective-permute-start | bytes 46088 | tf_op jit(solution)/shard_map/ppermute | solution.py:25
  124.3 6.9 %collective-permute-start.21 = (f32[3,10,1,128]{3,2,1,0:T(1,128)S(1)}, f32[3,10,1,128]{3,2,1,0:T(1,128)S(1)}, u32[]{:S(2)}, u32[]{:S(2)}) collective-permute-start(f32[3,10,1,128]{3,2,1,0:T(1,128)S(1)} %get-tuple-element.34), channel_id=1, source_target_pairs={{0,8},{8,16},{16,24},{1,9},{9,17},{17,25},{2,10},{10,18},{18,26},{... | collective-permute-start | bytes 46088 | tf_op jit(solution)/shard_map/ppermute | solution.py:24
  132.1 16.2 %collective-permute-start.22 = (f32[3,10,10,1]{3,2,1,0:T(8,128)}, f32[3,10,10,1]{3,2,1,0:T(8,128)S(1)}, u32[]{:S(2)}, u32[]{:S(2)}) collective-permute-start(f32[3,10,10,1]{3,2,1,0:T(8,128)} %get-tuple-element.18), channel_id=1, source_target_pairs={{1,0},{2,1},{3,2},{4,3},{5,4},{6,5},{7,6},{9,8},{10,9},{11,10},{12... | collective-permute-start | bytes 3608 | tf_op jit(solution)/shard_map/ppermute | solution.py:25
  133.4 14.9 %collective-permute-start.23 = (f32[3,10,10,1]{3,2,1,0:T(8,128)S(1)}, f32[3,10,10,1]{3,2,1,0:T(8,128)S(1)}, u32[]{:S(2)}, u32[]{:S(2)}) collective-permute-start(f32[3,10,10,1]{3,2,1,0:T(8,128)S(1)} %get-tuple-element.19), channel_id=1, source_target_pairs={{0,1},{1,2},{2,3},{3,4},{4,5},{5,6},{6,7},{8,9},{9,10},{10,11},{11... | collective-permute-start | bytes 3608 | tf_op jit(solution)/shard_map/ppermute | solution.py:24
  138.1 17.6 %all-to-all-start.1 = ((f32[8,8,3,128]{3,1,2,0:T(8,128)}), f32[8,8,3,128]{3,1,2,0:T(8,128)S(1)}, u32[]{:S(2)}, u32[]{:S(2)}) async-start(f32[8,8,3,128]{3,1,2,0:T(8,128)} %broadcast_in_dim.46), calls=%async_computation.1 | async-start | bytes 196608 | tf_op jit(solution)/shard_map/all_to_all | solution.py:86
  156.5 10.6 %all-to-all-start.2 = ((f32[4,8,8,3,128]{4,2,3,1,0:T(8,128)}), f32[4,8,8,3,128]{4,2,3,1,0:T(8,128)S(1)}, u32[]{:S(2)}, u32[]{:S(2)}) async-start(f32[4,8,8,3,128]{4,2,3,1,0:T(8,128)} %broadcast_in_dim.47), calls=%async_computation.2 | async-start | bytes 786432 | tf_op jit(solution)/shard_map/all_to_all | solution.py:86
  167.1 8.2 %collective-permute-start.24 = (f32[4,8,8,3,128]{4,2,3,1,0:T(8,128)S(1)}, f32[4,8,8,3,128]{4,2,3,1,0:T(8,128)S(1)}, u32[]{:S(2)}, u32[]{:S(2)}) collective-permute-start(f32[4,8,8,3,128]{4,2,3,1,0:T(8,128)S(1)} %all-to-all-done.2), channel_id=1, source_target_pairs={{0,32},{32,0},{1,33},{33,1},{2,34},{34,2},{3,35},{35,3},{4,36},{36... | collective-permute-start | bytes 1179656 | tf_op jit(solution)/shard_map/ppermute | solution.py:93
  (9 other events, 170.8 us)

commit v2 on v1

v2 whole, which is shorter than its diff:
```python
import jax
import jax.numpy as jnp
from jax import lax
from jax.experimental import pallas as pl
from jax.experimental.pallas import tpu as pltpu
from jax.sharding import PartitionSpec as P

RANK = 8
CLUST = 32
GX = ("x", "yl", "c")
ALL = GX + ("gy", "gz")
F32 = jnp.float32
HIGHEST = lax.Precision.HIGHEST

time_step = 0.1
softening = 0.4

FIELDS = 12
REACH = (4,) * 6 + (3,) * 4 + (2,) * 2
SIDE = 8
DEEP = 4
WIDE = SIDE + 2 * DEEP

X_TILES = [
    (f, d, yt) for f in range(FIELDS) for d in range(1, REACH[f] + 1) for yt in (0, 1) if d + yt <= REACH[f]
]
X_AT = {t: i for i, t in enumerate(X_TILES)}


def beyond(x):
    return max(-x, x - (SIDE - 1), 0)


Z_TILES = [
    (f, x, yt)
    for f in range(FIELDS)
    for x in range(-DEEP, SIDE + DEEP)
    for yt in (0, 1)
    if beyond(x) + yt + 1 <= REACH[f]
]
Z_AT = {t: i for i, t in enumerate(Z_TILES)}
Z_PACKED = -(-len(Z_TILES) // 16)


def lanes():
    return lax.broadcasted_iota(jnp.int32, (8, 128), 1)


def rows():
    return lax.broadcasted_iota(jnp.int32, (8, 128), 0)


def call(body, outs, n_in, scratch=(), name=None, flops=1000000, vmem=4 << 20):
    spec = pl.BlockSpec(memory_space=pltpu.VMEM)
    return pl.pallas_call(
        body,
        out_shape=[jax.ShapeDtypeStruct(s, F32) for s in outs],
        in_specs=[spec] * n_in,
        out_specs=[spec] * len(outs),
        scratch_shapes=list(scratch),
        cost_estimate=pl.CostEstimate(flops=flops, bytes_accessed=flops, transcendentals=0),
        compiler_params=pltpu.CompilerParams(vmem_limit_bytes=vmem),
        name=name,
    )


def own(stress, velocity, coefficients, f, x):
    if f < 6:
        return stress[f, x]
    if f < 9:
        return velocity[f - 6, x]
    return coefficients[f - 9, x]


def traction_body(stress, cell, normal, traction):
    z = jnp.broadcast_to(cell[...] % 128, (8, 128))
    row = jnp.broadcast_to(cell[...] // 128, (8, 128))
    here = [row == rows() + 8 * x for x in range(SIDE)]
    picked = []
    for f in range(6):
        total = jnp.zeros((8, 128), F32)
        for x in range(SIDE):
            at = jnp.take_along_axis(stress[f, x], z, axis=1, mode="promise_in_bounds")
            total = total + jnp.where(here[x], at, 0.0)
        picked.append(jnp.sum(total, axis=0, keepdims=True))
    n = [normal[k : k + 1, :] for k in range(3)]
    for k, (a, b, c) in enumerate(((0, 5, 4), (5, 1, 3), (4, 3, 2))):
        traction[k : k + 1, :] = picked[a] * n[0] + picked[b] * n[1] + picked[c] * n[2]


def sides_body(stress, velocity, lame, shear, buoyancy, flags, coefficients, up, down):
    for x in range(SIDE):
        soften = jnp.where(flags[x] == 1, softening, 1.0).astype(F32)
        mu = shear[x]
        coefficients[0, x] = (0.5 * time_step) * buoyancy[x]
        coefficients[1, x] = (0.5 * time_step) * (lame[x] + (1.0 - soften) * (2.0 / 3.0) * mu)
        coefficients[2, x] = time_step * soften * mu
    low = rows() < 4
    for f in range(FIELDS):
        for p in range(SIDE // 2):
            a = own(stress, velocity, coefficients, f, 2 * p)
            b = own(stress, velocity, coefficients, f, 2 * p + 1)
            i = f * (SIDE // 2) + p
            down[i] = jnp.where(low, a, pltpu.roll(b, 4, 0))
            up[i] = jnp.where(low, pltpu.roll(a, 4, 0), b)


def widen_y_body(stress, velocity, coefficients, from_low, from_high, beside, up, down):
    low = rows() < 4
    for f in range(FIELDS):
        for p in range(SIDE // 2):
            i = f * (SIDE // 2) + p
            a, b = from_high[i], from_low[i]
            beside[f, 2 * p] = jnp.where(low, a, pltpu.roll(b, 4, 0))
            beside[f, 2 * p + 1] = jnp.where(low, pltpu.roll(a, 4, 0), b)
    for i, (f, d, yt) in enumerate(X_TILES):
        for x, out in ((SIDE - d, up), (d - 1, down)):
            out[i] = beside[f, x] if yt else own(stress, velocity, coefficients, f, x)


def wide_tile(refs, f, x, yt):
    stress, velocity, coefficients, beside, x_low, x_high = refs
    if x < 0:
        return x_low[X_AT[f, -x, yt]]
    if x >= SIDE:
        return x_high[X_AT[f, x - (SIDE - 1), yt]]
    return beside[f, x] if yt else own(stress, velocity, coefficients, f, x)


def ends_body(stress, velocity, coefficients, beside, x_low, x_high, packed):
    refs = (stress, velocity, coefficients, beside, x_low, x_high)
    slot = lanes() // 8
    for t in range(Z_PACKED):
        total = None
        for k, (f, x, yt) in enumerate(Z_TILES[16 * t : 16 * t + 16]):
            turned = pltpu.roll(wide_tile(refs, f, x, yt), (4 + 8 * k) % 128, 1)
            total = turned if total is None else jnp.where(slot == k, turned, total)
        packed[t] = total


def step_body(
    stress, velocity, coefficients, beside, x_low, x_high, z_low, z_high, stress_out, velocity_out, held
):
    refs = (stress, velocity, coefficients, beside, x_low, x_high)
    first = lanes() % 8 < 4
    for f in range(FIELDS):
        for x in range(-DEEP, SIDE + DEEP):
            for yt in (0, 1):
                if beyond(x) + yt <= REACH[f]:
                    held[f, x + DEEP, 2 * yt] = wide_tile(refs, f, x, yt)
    for t in range(Z_PACKED):
        both = jnp.where(first, z_low[t], z_high[t])
        for k, (f, x, yt) in enumerate(Z_TILES[16 * t : 16 * t + 16]):
            held[f, x + DEEP, 2 * yt + 1] = pltpu.roll(both, (124 - 8 * k) % 128, 1)

    top, bottom = rows() == 7, rows() == 0
    right, left = lanes() == 127, lanes() == 0

    def ring(near, far, axis, size, last, start):
        nu, fu = pltpu.roll(near, size - 1, axis), pltpu.roll(far, size - 1, axis)
        nd, fd = pltpu.roll(near, 1, axis), pltpu.roll(far, 1, axis)
        return (
            jnp.where(last, fu, nu) - jnp.where(start, fd, nd),
            jnp.where(last, nu, fu) - jnp.where(start, nd, fd),
        )

    def along_x(f, i, tiles):
        return {t: held[f, i + 1, t] - held[f, i - 1, t] for t in tiles}

    def along_y(f, i, tiles):
        out = {}
        for zt in (0, 1):
            if zt in tiles or zt + 2 in tiles:
                out[zt], out[zt + 2] = ring(held[f, i, zt], held[f, i, zt + 2], 0, 8, top, bottom)
        return out

    def along_z(f, i, tiles):
        out = {}
        for yt in (0, 2):
            if yt in tiles or yt + 1 in tiles:
                out[yt], out[yt + 1] = ring(held[f, i, yt], held[f, i, yt + 1], 1, 128, right, left)
        return out

    def speed(i, tiles):
        for k, (a, b, c) in enumerate(((0, 5, 4), (5, 1, 3), (4, 3, 2))):
            dx, dy, dz = along_x(a, i, tiles), along_y(b, i, tiles), along_z(c, i, tiles)
            for t in tiles:
                held[6 + k, i, t] = held[6 + k, i, t] + held[9, i, t] * (dx[t] + dy[t] + dz[t])

    def strain(i, tiles, put):
        xx, yy, zz = along_x(6, i, tiles), along_y(7, i, tiles), along_z(8, i, tiles)
        for t in tiles:
            iso = held[10, i, t] * (xx[t] + yy[t] + zz[t])
            scale = held[11, i, t]
            for f, e in ((0, xx), (1, yy), (2, zz)):
                put(f, i, t, held[f, i, t] + (iso + scale * e[t]))
        for f, one, other in (
            (3, along_z(7, i, tiles), along_y(8, i, tiles)),
            (4, along_z(6, i, tiles), along_x(8, i, tiles)),
            (5, along_y(6, i, tiles), along_x(7, i, tiles)),
        ):
            for t in tiles:
                put(f, i, t, held[f, i, t] + 0.5 * held[11, i, t] * (one[t] + other[t]))

    def keep(f, i, t, value):
        held[f, i, t] = value

    def hand_out(f, i, t, value):
        stress_out[f, i - DEEP] = value

    everything = (0, 1, 2, 3)

    def loop(start, stop, body):
        def step(i, carry):
            body(i)
            return carry

        lax.fori_loop(start, stop, step, 0)

    loop(1, WIDE - 1, lambda i: speed(i, everything))
    loop(2, WIDE - 2, lambda i: strain(i, everything, keep))
    loop(3, WIDE - 3, lambda i: speed(i, (0, 1, 2)))

    def last(i):
        strain(i, (0,), hand_out)
        for k in range(3):
            velocity_out[k, i - DEEP] = held[6 + k, i, 0]

    loop(DEEP, DEEP + SIDE, last)


def panels_body(core, mine, other, traction, near, far, basis, ranks, out, sums):
    n_x, n_y, n_z = mine.shape[0], mine.shape[1], mine.shape[2] // 3
    per_core = n_y // 2 * n_z
    c = core[0]
    for which, source in ((c, mine), (1 - c, other)):
        def cluster(i, carry, which=which, source=source):
            x, yl, half = i // 4, i // 2 % 2, i % 2
            totals = [jnp.zeros((8, 128), F32) for _ in range(3)]
            for g in range(2):
                block = source[x, (half * 2 + g) * 2 + yl]
                start = ((x * 2 + yl) * 2 + which) * per_core + (half * 2 + g) * n_z
                for z in range(n_z):
                    part = basis[:, pl.ds(pl.multiple_of((start + z) * 128, 128), 128)]
                    for k in range(3):
                        totals[k] = totals[k] + part * block[3 * z + k : 3 * z + k + 1, :]
            at = ((x * 2 + yl) * 2 + which) * 2 + half
            for k in range(3):
                sums[k, pl.ds(pl.multiple_of(at * RANK, RANK), RANK), :] = totals[k]
            return carry

        lax.fori_loop(0, n_x * 4, cluster, 0)
    last = (((1,), (1,)), ((), ()))
    ones = jnp.ones((8, 128), F32)
    rank_of = lax.broadcasted_iota(jnp.int32, (CLUST, CLUST * RANK), 1)
    cluster_of = lax.broadcasted_iota(jnp.int32, (CLUST, CLUST * RANK), 0)
    spread_out = (rank_of // RANK == cluster_of).astype(F32)
    limit = jnp.dot(
        jnp.broadcast_to(ranks[...].astype(F32), (8, CLUST)), spread_out, preferred_element_type=F32
    )
    rank = lax.broadcasted_iota(jnp.int32, (8, CLUST * RANK), 1) % RANK
    kept = rank.astype(F32) + 0.5 < limit
    row = lax.broadcasted_iota(jnp.int32, (8, CLUST * RANK), 0)
    projected = jnp.zeros((8, CLUST * RANK), F32)
    for k in range(3):
        total = lax.dot_general(ones, sums[k], last, precision=HIGHEST, preferred_element_type=F32)
        projected = jnp.where(kept & (row == k), total, projected)
    far_term = lax.dot_general(projected, far[...], last, precision=HIGHEST, preferred_element_type=F32)
    near_term = lax.dot_general(traction[...], near[...], last, precision=HIGHEST, preferred_element_type=F32)
    out[...] = near_term + far_term[0:3, :]


def both_ways(up, down, axis):
    peers = lax.axis_size(axis)
    rising = [(i, i + 1) for i in range(peers - 1)]
    falling = [(j, i) for i, j in rising]
    return lax.ppermute(up, axis, rising), lax.ppermute(down, axis, falling)


def spread(x, axes):
    peers = lax.axis_size(axes)
    return lax.all_to_all(jnp.broadcast_to(x[None], (peers,) + x.shape), axes, 0, 0)


def after(x, *others):
    return lax.optimization_barrier((x,) + others)[0]


def per_device(
    stress,
    velocity,
    lame_lambda,
    shear_modulus,
    buoyancy,
    yield_flags,
    panel_cell,
    panel_normal,
    near_block,
    far_rows,
    far_basis,
    block_ranks,
):
    tile = (SIDE, 128)
    (traction,) = call(traction_body, [(3, 128)], 3, name="traction")(
        stress, panel_cell.reshape(1, 128), panel_normal
    )
    half = (FIELDS * SIDE // 2,) + tile
    coefficients, up, down = call(sides_body, [(3, SIDE) + tile, half, half], 6, name="sides")(
        stress, velocity, lame_lambda, shear_modulus, buoyancy, yield_flags
    )
    y_low, y_high = both_ways(up, down, "gy")
    block = spread(after(traction, up, down), "gz")
    x_message = (len(X_TILES),) + tile
    beside, up, down = call(
        widen_y_body, [(FIELDS, SIDE) + tile, x_message, x_message], 5, name="widen_y"
    )(stress, velocity, coefficients, y_low, y_high)
    x_low, x_high = both_ways(up, down, GX)
    block = spread(after(block.reshape(-1, 128), up, down), ("gy", "yl"))
    (packed,) = call(ends_body, [(Z_PACKED,) + tile], 6, name="ends")(
        stress, velocity, coefficients, beside, x_low, x_high
    )
    z_low, z_high = both_ways(packed, packed, "gz")
    block = spread(after(block, packed), "x")
    other = lax.ppermute(block, "c", [(0, 1), (1, 0)])
    stress_out, velocity_out = call(
        step_body,
        [stress.shape, velocity.shape],
        8,
        scratch=[pltpu.VMEM((FIELDS, WIDE, 4) + tile, F32)],
        name="step",
        flops=20000000,
        vmem=8 << 20,
    )(stress, velocity, coefficients, beside, x_low, x_high, z_low, z_high)
    displacement = panels(block, other, traction, near_block, far_rows, far_basis, block_ranks, lax.axis_index("c"))
    return stress_out, velocity_out, displacement


def panels(block, other, traction, near_block, far_rows, far_basis, block_ranks, core):
    spec = pl.BlockSpec(memory_space=pltpu.VMEM)
    return pl.pallas_call(
        panels_body,
        out_shape=jax.ShapeDtypeStruct((3, 128), F32),
        in_specs=[pl.BlockSpec(memory_space=pltpu.SMEM)] + [spec] * 7,
        out_specs=spec,
        scratch_shapes=[pltpu.VMEM((3, CLUST * RANK, 128), F32)],
        cost_estimate=pl.CostEstimate(flops=3000000, bytes_accessed=3000000, transcendentals=0),
        compiler_params=pltpu.CompilerParams(vmem_limit_bytes=8 << 20),
        name="panels",
    )(core.astype(jnp.int32).reshape(1), block, other, traction, near_block, far_rows, far_basis, block_ranks)


def solution(mesh):
    shape = dict(mesh.shape)
    fine = jax.sharding.Mesh(
        mesh.devices.reshape(shape["gx"] // 4, 2, 2, shape["gy"], shape["gz"]), ALL
    )
    zones = P(GX, "gy", "gz")
    fields = P(None, GX, "gy", "gz")
    return jax.shard_map(
        per_device,
        mesh=fine,
        in_specs=(
            fields,
            fields,
            zones,
            zones,
            zones,
            zones,
            P(ALL),
            P(None, ALL),
            P(ALL, None),
            P(ALL, None),
            P(ALL, None),
            P(ALL, None),
        ),
        out_specs=(fields, fields, P(None, ALL)),
        check_vma=False,
    )
```

time: 184 us -> 102 us (0.55)
  starting transfers between devices: 116 us -> 30 us
  blocking collectives: 0 us -> 26.1 us
  waiting for transfers between devices: 39 us -> 19.4 us
  Pallas kernels: 0 us -> 10.7 us
  other arithmetic: 7.55 us -> 0 us
  matrix products: 5.65 us -> 0 us
    ppermute x25 -> x7, starting transfers between devices: 88.1 us -> 23.9 us  [the longest x6 16.7 us: both_ways(): return (lax.ppermute(up, axis, rising), lax.ppermute(down, axis, falling))]
    all_to_all x0 -> x2, blocking collectives: none -> 26.1 us  [spread(): lax.all_to_all(jnp.broadcast_to(x[None], (peers,) + x.shape), axes, 0, 0)]
    all_to_all x3 -> x1, starting transfers between devices: 28.3 us -> 6.12 us  [spread(): lax.all_to_all(jnp.broadcast_to(x[None], (peers,) + x.shape), axes, 0, 0)]
    ppermute x25 -> x7, waiting for transfers between devices: 28.8 us -> 14.7 us  [the longest x6 14.7 us: both_ways(): return (lax.ppermute(up, axis, rising), lax.ppermute(down, axis, falling))]
    pallas_call x0 -> x6, Pallas kernels: none -> 10.7 us  [the longest x1 6.27 us: per_device(): call(step_body, [stress.shape, velocity.shape], 8, scratch=[pltpu.VMEM((F...]
    unnamed x29 -> x42, local copies, waits for them, and re-layouts: 3.79 us -> 13.3 us
    dot_general x3 -> x0, matrix products: 5.65 us -> none  [the longest x1 4.68 us: per_device(): jnp.einsum('rcp,kcp->crk', basis, grouped, precision=lax.Precision.HIGHEST)]
    all_to_all x3 -> x1, waiting for transfers between devices: 10.2 us -> 4.73 us  [spread(): lax.all_to_all(jnp.broadcast_to(x[None], (peers,) + x.shape), axes, 0, 0)]
  transfers between devices with their start and end apart: 28 -> 8, of which waited for: 13 -> 5; matrix products, arithmetic and copies ran while one was open for 8% -> 1% of each run, Pallas kernels for 0% -> 7%
where the time goes in v2:
time: 102 us; the launch traced here: 101 us
  starting transfers between devices  30 us (29%)
  blocking collectives  26.1 us (26%)
  waiting for transfers between devices  19.4 us (19%)
  local copies, waits for them, and re-layouts  14 us (14%)
  Pallas kernels  10.7 us (10%)
    all_to_all x2, blocking collectives, spread(): lax.all_to_all(jnp.broadcast_to(x[None], (peers,) + x.shape), axes, 0, 0)  26.1 us
    ppermute x6, starting transfers between devices, both_ways(): return (lax.ppermute(up, axis, rising), lax.ppermute(down, axis, falling))  16.7 us
    ppermute x6, waiting for transfers between devices, both_ways(): return (lax.ppermute(up, axis, rising), lax.ppermute(down, axis, falling))  14.7 us
    unnamed x42, local copies, waits for them, and re-layouts  13.3 us
    ppermute x1, starting transfers between devices, per_device(): other = lax.ppermute(block, 'c', [(0, 1), (1, 0)])  7.12 us
    pallas_call x1, Pallas kernels, per_device(): call(step_body, [stress.shape, velocity.shape], 8, scratch=[pltpu.VMEM((F...  6.27 us
    all_to_all x1, starting transfers between devices, spread(): lax.all_to_all(jnp.broadcast_to(x[None], (peers,) + x.shape), axes, 0, 0)  6.12 us
    all_to_all x1, waiting for transfers between devices, spread(): lax.all_to_all(jnp.broadcast_to(x[None], (peers,) + x.shape), axes, 0, 0)  4.73 us
  transfers between devices with their start and end apart: 8, of which 5 were waited for; matrix products, arithmetic and copies ran while one was open for 1% of the time, Pallas kernels for 7%

profile of v2, /device:TPU:1, one launch (start us, length us, event | category | flops | bytes accessed | tf_op | source)
XLA Modules:
  0.0 101.0 jit_solution(455188328485612979)
XLA Ops:
  0.6 0.9 copy-done
  1.6 0.9 copy-done.4
  2.5 0.8 copy-done.12
  3.2 0.8 copy-done.13
  4.0 0.8 copy-done.14
  4.7 0.8 copy-done.15
  5.6 5.2 %collective-permute-start = (f32[48,8,128]{2,1,0:T(8,128)S(1)}, f32[48,8,128]{2,1,0:T(8,128)S(1)}, u32[]{:S(2)}, u32[]{:S(2)}) collective-permute-start(f32[48,8,128]{2,1,0:T(8,128)S(1)} %get-tuple-element.15), channel_id=1, source_target_pairs={{0,8},{8,16},{16,24},{1,9},{9,17},{17,25},{2,10},{10,18},{18,26},{... | collective-permute-start | bytes 589832 | tf_op jit(solution)/shard_map/ppermute | solution.py:277
  10.8 1.3 %collective-permute-start.1 = (f32[48,8,128]{2,1,0:T(8,128)S(1)}, f32[48,8,128]{2,1,0:T(8,128)S(1)}, u32[]{:S(2)}, u32[]{:S(2)}) collective-permute-start(f32[48,8,128]{2,1,0:T(8,128)S(1)} %get-tuple-element.16), channel_id=1, source_target_pairs={{8,0},{16,8},{24,16},{9,1},{17,9},{25,17},{10,2},{18,10},{26,18},{... | collective-permute-start | bytes 589832 | tf_op jit(solution)/shard_map/ppermute | solution.py:277
  12.1 1.3 %collective-permute-done.from_low = f32[48,8,128]{2,1,0:T(8,128)S(1)} collective-permute-done((f32[48,8,128]{2,1,0:T(8,128)S(1)}, f32[48,8,128]{2,1,0:T(8,128)S(1)}, u32[]{:S(2)}, u32[]{:S(2)}) %collective-permute-start) | collective-permute-done | bytes 196640 | tf_op jit(solution)/shard_map/ppermute | solution.py:277
  13.4 12.3 %collective-permute-done.1.from_high = f32[48,8,128]{2,1,0:T(8,128)S(1)} collective-permute-done((f32[48,8,128]{2,1,0:T(8,128)S(1)}, f32[48,8,128]{2,1,0:T(8,128)S(1)}, u32[]{:S(2)}, u32[]{:S(2)}) %collective-permute-start.1) | collective-permute-done | bytes 196640 | tf_op jit(solution)/shard_map/ppermute | solution.py:277
  25.7 1.9 %collective-permute-start.2 = (f32[68,8,128]{2,1,0:T(8,128)S(1)}, f32[68,8,128]{2,1,0:T(8,128)S(1)}, u32[]{:S(2)}, u32[]{:S(2)}) collective-permute-start(f32[68,8,128]{2,1,0:T(8,128)S(1)} %get-tuple-element.18), channel_id=1, source_target_pairs={{0,32},{32,64},{64,96},{96,128},{128,160},{160,192},{192,224},{224... | collective-permute-start | bytes 835592 | tf_op jit(solution)/shard_map/ppermute | solution.py:277
  27.6 2.4 %collective-permute-start.3 = (f32[68,8,128]{2,1,0:T(8,128)S(1)}, f32[68,8,128]{2,1,0:T(8,128)S(1)}, u32[]{:S(2)}, u32[]{:S(2)}) collective-permute-start(f32[68,8,128]{2,1,0:T(8,128)S(1)} %get-tuple-element.19), channel_id=1, source_target_pairs={{32,0},{64,32},{96,64},{128,96},{160,128},{192,160},{224,192},{256... | collective-permute-start | bytes 835592 | tf_op jit(solution)/shard_map/ppermute | solution.py:277
  30.1 0.7 copy-done.18
  30.7 0.7 copy-done.19
  32.1 16.4 %all_to_all.15 = f32[8,3,128]{2,1,0:T(4,128)S(1)} all-to-all(f32[8,3,128]{2,1,0:T(4,128)S(1)} %broadcast_in_dim.6), channel_id=1, replica_groups=mesh['x'=4,'yl'=2,'c'=2,'gy'=4,'gz'=8] {'gz'}, dimensions={0} | all-to-all | bytes 24576 | tf_op jit(solution)/shard_map/all_to_all | solution.py:282
  48.6 0.7 broadcast_in_dim.7
  49.2 6.1 %all-to-all-start.1 = ((f32[8,24,128]{2,1,0:T(8,128)}), f32[8,24,128]{2,1,0:T(8,128)S(1)}, u32[]{:S(2)}, u32[]{:S(2)}) async-start(f32[8,24,128]{2,1,0:T(8,128)} %broadcast_in_dim.7), calls=%async_computation.1 | async-start | bytes 196608 | tf_op jit(solution)/shard_map/all_to_all | solution.py:282
  55.4 1.0 %copy-done.1 = f32[6,8,8,128]{3,2,1,0:T(8,128)S(1)} copy-done((f32[6,8,8,128]{3,2,1,0:T(8,128)S(1)}, f32[6,8,8,128]{3,2,1,0:T(8,128)}, u32[]{:S(2)}) %copy-start.1) | copy-done | bytes 196632
  56.4 0.9 copy-done.5
  58.3 4.7 %all-to-all-done.1 = f32[8,24,128]{2,1,0:T(8,128)S(1)} async-done(((f32[8,24,128]{2,1,0:T(8,128)}), f32[8,24,128]{2,1,0:T(8,128)S(1)}, u32[]{:S(2)}, u32[]{:S(2)}) %all-to-all-start.1) | async-done | bytes 98336 | tf_op jit(solution)/shard_map/all_to_all | solution.py:282
  63.1 9.7 %all_to_all.16.mine = f32[4,8,24,128]{3,2,1,0:T(8,128)S(1)} all-to-all(f32[4,8,24,128]{3,2,1,0:T(8,128)S(1)} %broadcast_in_dim.8), channel_id=1, replica_groups=mesh['x'=4,'yl'=2,'c'=2,'gy'=4,'gz'=8] {'x'}, dimensions={0} | all-to-all | bytes 786432 | tf_op jit(solution)/shard_map/all_to_all | solution.py:282
  72.7 7.1 %collective-permute-start.6 = (f32[4,8,24,128]{3,2,1,0:T(8,128)S(1)}, f32[4,8,24,128]{3,2,1,0:T(8,128)}, u32[]{:S(2)}, u32[]{:S(2)}) collective-permute-start(f32[4,8,24,128]{3,2,1,0:T(8,128)S(1)} %all_to_all.16.mine), channel_id=1, source_target_pairs={{0,32},{32,0},{1,33},{33,1},{2,34},{34,2},{3,35},{35,3},{4,36},{36... | collective-permute-start | bytes 1179656 | tf_op jit(solution)/shard_map/ppermute | solution.py:324
  79.8 1.3 %collective-permute-start.5 = (f32[18,8,128]{2,1,0:T(8,128)}, f32[18,8,128]{2,1,0:T(8,128)}, u32[]{:S(2)}, u32[]{:S(2)}) collective-permute-start(f32[18,8,128]{2,1,0:T(8,128)} %copy-done.10), channel_id=1, source_target_pairs={{1,0},{2,1},{3,2},{4,3},{5,4},{6,5},{7,6},{9,8},{10,9},{11,10},{12... | collective-permute-start | bytes 221192 | tf_op jit(solution)/shard_map/ppermute | solution.py:277
  81.1 4.6 %collective-permute-start.4 = (f32[18,8,128]{2,1,0:T(8,128)}, f32[18,8,128]{2,1,0:T(8,128)}, u32[]{:S(2)}, u32[]{:S(2)}) collective-permute-start(f32[18,8,128]{2,1,0:T(8,128)} %copy-done.10), channel_id=1, source_target_pairs={{0,1},{1,2},{2,3},{3,4},{4,5},{5,6},{6,7},{8,9},{9,10},{10,11},{11... | collective-permute-start | bytes 221192 | tf_op jit(solution)/shard_map/ppermute | solution.py:277
  85.9 0.9 collective-permute-done.4.z_low
  86.8 1.0 copy-done.8
  87.8 6.3 %step.1 = (f32[6,8,8,128]{3,2,1,0:T(8,128)}, f32[3,8,8,128]{3,2,1,0:T(8,128)}) custom-call(f32[6,8,8,128]{3,2,1,0:T(8,128)S(1)} %copy-done.2, f32[3,8,8,128]{3,2,1,0:T(8,128)S(1)} %copy-done.6, f32[3,8,8,128]{3,2,1,0:T(8,128)S(1)} %get-tuple-element.14.coefficients, f32[12,8,8,128]{3,2,1,0:T(8,128)S(1)} %get-tuple-element.17.beside, ...), custom_call_target="tpu_custom_call" | custom-call | flops 20000000 | bytes 20000000 | tf_op jit(solution)/shard_map/step/pallas_call | solution.py:325
  94.1 0.9 copy-done.9
  95.0 0.8 copy-done.11
  95.8 0.7 copy-done.17
  96.5 0.7 copy-done.20
  97.2 3.9 %panels.1 = f32[3,128]{1,0:T(4,128)} custom-call(s32[1]{0:T(128)} %bitcast.core, f32[4,8,24,128]{3,2,1,0:T(8,128)S(1)} %all_to_all.16.mine, f32[4,8,24,128]{3,2,1,0:T(8,128)} %collective-permute-done.6.other, f32[3,128]{1,0:T(4,128)S(1)} %copy-done.17, f32[128,128]{1,0:T(8,128)S(1)} %copy-done.11, f32[128,256]{1,0:T(8,128)S(1)} %copy-done.9, ...), custom_call_target="tpu_custom_call" | custom-call | flops 3000000 | bytes 3000000 | tf_op jit(solution)/shard_map/panels/pallas_call | solution.py:340
  (38 shorter events, 2.1 us)
Async XLA Ops:
  0.6 0.9 copy-start
  1.6 0.9 copy-start.4
  2.5 0.8 copy-start.12
  3.2 0.8 copy-start.13
  4.0 0.8 copy-start.14
  4.7 0.8 copy-start.15
  5.5 81.3 %copy-start.2 = (f32[6,8,8,128]{3,2,1,0:T(8,128)S(1)}, f32[6,8,8,128]{3,2,1,0:T(8,128)}, u32[]{:S(2)}) copy-start(f32[6,8,8,128]{3,2,1,0:T(8,128)} %stress.9) | copy-start | bytes 589828
  5.5 81.3 %copy-start.6 = (f32[3,8,8,128]{3,2,1,0:T(8,128)S(1)}, f32[3,8,8,128]{3,2,1,0:T(8,128)}, u32[]{:S(2)}) copy-start(f32[3,8,8,128]{3,2,1,0:T(8,128)} %velocity.7) | copy-start | bytes 294916
  5.6 7.8 %collective-permute-start = (f32[48,8,128]{2,1,0:T(8,128)S(1)}, f32[48,8,128]{2,1,0:T(8,128)S(1)}, u32[]{:S(2)}, u32[]{:S(2)}) collective-permute-start(f32[48,8,128]{2,1,0:T(8,128)S(1)} %get-tuple-element.15), channel_id=1, source_target_pairs={{0,8},{8,16},{16,24},{1,9},{9,17},{17,25},{2,10},{10,18},{18,26},{... | collective-permute-start | bytes 589832 | tf_op jit(solution)/shard_map/ppermute | solution.py:277
  10.8 14.9 %collective-permute-start.1 = (f32[48,8,128]{2,1,0:T(8,128)S(1)}, f32[48,8,128]{2,1,0:T(8,128)S(1)}, u32[]{:S(2)}, u32[]{:S(2)}) collective-permute-start(f32[48,8,128]{2,1,0:T(8,128)S(1)} %get-tuple-element.16), channel_id=1, source_target_pairs={{8,0},{16,8},{24,16},{9,1},{17,9},{25,17},{10,2},{18,10},{26,18},{... | collective-permute-start | bytes 589832 | tf_op jit(solution)/shard_map/ppermute | solution.py:277
  25.7 29.7 %collective-permute-start.2 = (f32[68,8,128]{2,1,0:T(8,128)S(1)}, f32[68,8,128]{2,1,0:T(8,128)S(1)}, u32[]{:S(2)}, u32[]{:S(2)}) collective-permute-start(f32[68,8,128]{2,1,0:T(8,128)S(1)} %get-tuple-element.18), channel_id=1, source_target_pairs={{0,32},{32,64},{64,96},{96,128},{128,160},{160,192},{192,224},{224... | collective-permute-start | bytes 835592 | tf_op jit(solution)/shard_map/ppermute | solution.py:277
  27.6 27.7 %collective-permute-start.3 = (f32[68,8,128]{2,1,0:T(8,128)S(1)}, f32[68,8,128]{2,1,0:T(8,128)S(1)}, u32[]{:S(2)}, u32[]{:S(2)}) collective-permute-start(f32[68,8,128]{2,1,0:T(8,128)S(1)} %get-tuple-element.19), channel_id=1, source_target_pairs={{32,0},{64,32},{96,64},{128,96},{160,128},{192,160},{224,192},{256... | collective-permute-start | bytes 835592 | tf_op jit(solution)/shard_map/ppermute | solution.py:277
  30.0 0.7 copy-start.18
  30.7 0.7 copy-start.19
  31.5 0.6 copy-start.16
  49.2 13.8 %all-to-all-start.1 = ((f32[8,24,128]{2,1,0:T(8,128)}), f32[8,24,128]{2,1,0:T(8,128)S(1)}, u32[]{:S(2)}, u32[]{:S(2)}) async-start(f32[8,24,128]{2,1,0:T(8,128)} %broadcast_in_dim.7), calls=%async_computation.1 | async-start | bytes 196608 | tf_op jit(solution)/shard_map/all_to_all | solution.py:282
  55.4 7.7 %copy-start.7 = (f32[68,8,128]{2,1,0:T(8,128)}, f32[68,8,128]{2,1,0:T(8,128)S(1)}, u32[]{:S(2)}) copy-start(f32[68,8,128]{2,1,0:T(8,128)S(1)} %collective-permute-done.3.x_high) | copy-start | bytes 835588
  55.4 1.0 %copy-start.1 = (f32[6,8,8,128]{3,2,1,0:T(8,128)S(1)}, f32[6,8,8,128]{3,2,1,0:T(8,128)}, u32[]{:S(2)}) copy-start(f32[6,8,8,128]{3,2,1,0:T(8,128)} %stress.9) | copy-start | bytes 589828
  56.4 0.9 copy-start.5
  57.3 36.8 %copy-start.3 = (f32[8,65536]{1,0:T(8,128)S(1)}, f32[8,65536]{1,0:T(8,128)}, u32[]{:S(2)}) copy-start(f32[8,65536]{1,0:T(8,128)} %basis.1) | copy-start | bytes 6291460
  57.7 0.6 copy-start.10
  72.7 21.4 %collective-permute-start.6 = (f32[4,8,24,128]{3,2,1,0:T(8,128)S(1)}, f32[4,8,24,128]{3,2,1,0:T(8,128)}, u32[]{:S(2)}, u32[]{:S(2)}) collective-permute-start(f32[4,8,24,128]{3,2,1,0:T(8,128)S(1)} %all_to_all.16.mine), channel_id=1, source_target_pairs={{0,32},{32,0},{1,33},{33,1},{2,34},{34,2},{3,35},{35,3},{4,36},{36... | collective-permute-start | bytes 1179656 | tf_op jit(solution)/shard_map/ppermute | solution.py:324
  79.8 6.1 %collective-permute-start.5 = (f32[18,8,128]{2,1,0:T(8,128)}, f32[18,8,128]{2,1,0:T(8,128)}, u32[]{:S(2)}, u32[]{:S(2)}) collective-permute-start(f32[18,8,128]{2,1,0:T(8,128)} %copy-done.10), channel_id=1, source_target_pairs={{1,0},{2,1},{3,2},{4,3},{5,4},{6,5},{7,6},{9,8},{10,9},{11,10},{12... | collective-permute-start | bytes 221192 | tf_op jit(solution)/shard_map/ppermute | solution.py:277
  81.1 5.7 %collective-permute-start.4 = (f32[18,8,128]{2,1,0:T(8,128)}, f32[18,8,128]{2,1,0:T(8,128)}, u32[]{:S(2)}, u32[]{:S(2)}) collective-permute-start(f32[18,8,128]{2,1,0:T(8,128)} %copy-done.10), channel_id=1, source_target_pairs={{0,1},{1,2},{2,3},{3,4},{4,5},{5,6},{6,7},{8,9},{9,10},{10,11},{11... | collective-permute-start | bytes 221192 | tf_op jit(solution)/shard_map/ppermute | solution.py:277
  86.8 1.0 copy-start.8
  94.1 0.9 copy-start.9
  95.0 0.8 copy-start.11
  95.8 0.7 copy-start.17
  96.5 0.7 copy-start.20

commit v3 on v2

v3 whole, which is shorter than its diff:
```python
import jax
import jax.numpy as jnp
from jax import lax
from jax.experimental import pallas as pl
from jax.experimental.pallas import tpu as pltpu
from jax.sharding import PartitionSpec as P

RANK = 8
CLUST = 32
GX = ("x", "yl", "c")
ALL = GX + ("gy", "gz")
F32 = jnp.float32
HIGHEST = lax.Precision.HIGHEST

FIRST = 56 << 20
time_step = 0.1
softening = 0.4

FIELDS = 12
REACH = (4,) * 6 + (3,) * 4 + (2,) * 2
SIDE = 8
DEEP = 4
WIDE = SIDE + 2 * DEEP

X_TILES = [
    (f, d, yt) for f in range(FIELDS) for d in range(1, REACH[f] + 1) for yt in (0, 1) if d + yt <= REACH[f]
]
X_AT = {t: i for i, t in enumerate(X_TILES)}


def beyond(x):
    return max(-x, x - (SIDE - 1), 0)


Z_TILES = [
    (f, x, yt)
    for f in range(FIELDS)
    for x in range(-DEEP, SIDE + DEEP)
    for yt in (0, 1)
    if beyond(x) + yt + 1 <= REACH[f]
]
Z_AT = {t: i for i, t in enumerate(Z_TILES)}
Z_PACKED = -(-len(Z_TILES) // 16)


def lanes():
    return lax.broadcasted_iota(jnp.int32, (8, 128), 1)


def rows():
    return lax.broadcasted_iota(jnp.int32, (8, 128), 0)


def call(body, outs, specs, scratch=(), name=None, flops=1000000, vmem=4 << 20, in_place=None):
    spec = pl.BlockSpec(memory_space=pltpu.VMEM)
    return pl.pallas_call(
        body,
        out_shape=[s if hasattr(s, "dtype") else jax.ShapeDtypeStruct(s, F32) for s in outs],
        in_specs=[pl.BlockSpec(memory_space=m) for m in specs],
        out_specs=[spec] * len(outs),
        scratch_shapes=list(scratch),
        cost_estimate=pl.CostEstimate(flops=flops, bytes_accessed=flops, transcendentals=0),
        compiler_params=pltpu.CompilerParams(vmem_limit_bytes=vmem),
        input_output_aliases=in_place or {},
        name=name,
    )


def odd(axis):
    return lax.axis_index(axis) % 2


def swapped(parity, a, b):
    return jnp.where(parity == 0, a, b), jnp.where(parity == 0, b, a)


def first_body(
    stress, velocity, lame, shear, buoyancy, flags, cell, normal, near, far, ranks,
    fields, traction, one, two, near_out, far_out, ranks_out,
    lame_in, shear_in, buoyancy_in, flags_in, cell_in, normal_in, sems,
):
    copies = [
        pltpu.make_async_copy(source, target, sems.at[i])
        for i, (source, target) in enumerate(
            (
                (stress, fields.at[0:6]),
                (cell, cell_in),
                (normal, normal_in),
                (velocity, fields.at[6:9]),
                (lame, lame_in),
                (shear, shear_in),
                (buoyancy, buoyancy_in),
                (flags, flags_in),
                (near, near_out),
                (far, far_out),
                (ranks, ranks_out),
            )
        )
    ]
    for copy in copies:
        copy.start()
    for copy in copies[3:8]:
        copy.wait()
    for x in range(SIDE):
        soften = jnp.where(flags_in[x] == 1, softening, 1.0).astype(F32)
        mu = shear_in[x]
        fields[9, x] = (0.5 * time_step) * buoyancy_in[x]
        fields[10, x] = (0.5 * time_step) * (lame_in[x] + (1.0 - soften) * (2.0 / 3.0) * mu)
        fields[11, x] = time_step * soften * mu
    for copy in copies[:3]:
        copy.wait()
    z = jnp.broadcast_to(cell_in[...] % 128, (8, 128))
    row = jnp.broadcast_to(cell_in[...] // 128, (8, 128))
    here = [row == rows() + 8 * x for x in range(SIDE)]
    picked = []
    for f in range(6):
        total = jnp.zeros((8, 128), F32)
        for x in range(SIDE):
            at = jnp.take_along_axis(fields[f, x], z, axis=1, mode="promise_in_bounds")
            total = total + jnp.where(here[x], at, 0.0)
        picked.append(jnp.sum(total, axis=0, keepdims=True))
    n = [normal_in[k : k + 1, :] for k in range(3)]
    for k, (a, b, c) in enumerate(((0, 5, 4), (5, 1, 3), (4, 3, 2))):
        value = picked[a] * n[0] + picked[b] * n[1] + picked[c] * n[2]
        for peer in range(traction.shape[0]):
            traction[peer, k : k + 1, :] = value
    low = rows() < 4
    for f in range(FIELDS):
        for p in range(SIDE // 2):
            a, b = fields[f, 2 * p], fields[f, 2 * p + 1]
            i = f * (SIDE // 2) + p
            down = jnp.where(low, a, pltpu.roll(b, 4, 0))
            up = jnp.where(low, pltpu.roll(a, 4, 0), b)
            one[i], two[i] = swapped(odd("gy"), up, down)
    for copy in copies[8:]:
        copy.wait()


def widen_y_body(fields, from_one, from_two, block, beside, one, two, copies):
    low = rows() < 4
    for f in range(FIELDS):
        for p in range(SIDE // 2):
            i = f * (SIDE // 2) + p
            a, b = swapped(odd("gy"), from_one[i], from_two[i])
            beside[f, 2 * p] = jnp.where(low, a, pltpu.roll(b, 4, 0))
            beside[f, 2 * p + 1] = jnp.where(low, pltpu.roll(a, 4, 0), b)
    for i, (f, d, yt) in enumerate(X_TILES):
        source = beside if yt else fields
        one[i], two[i] = swapped(odd("c"), source[f, SIDE - d], source[f, d - 1])
    whole = jnp.concatenate([block[z] for z in range(block.shape[0])], axis=0)
    for peer in range(copies.shape[0]):
        copies[peer] = whole


def wide_tile(refs, f, x, yt):
    fields, beside, from_one, from_two = refs
    if beyond(x):
        i = X_AT[f, beyond(x), yt]
        return swapped(odd("c"), from_one[i], from_two[i])[x < 0]
    return beside[f, x] if yt else fields[f, x]


def ends_body(fields, beside, from_one, from_two, block, packed, wide, copies):
    refs = (fields, beside, from_one, from_two)
    for f in range(FIELDS):
        for x in range(-DEEP, SIDE + DEEP):
            for yt in (0, 1):
                if beyond(x) + yt <= REACH[f]:
                    wide[f, x + DEEP, yt] = wide_tile(refs, f, x, yt)
    slot = lanes() // 8
    for t in range(Z_PACKED):
        total = None
        for k, (f, x, yt) in enumerate(Z_TILES[16 * t : 16 * t + 16]):
            turned = pltpu.roll(wide[f, x + DEEP, yt], (4 + 8 * k) % 128, 1)
            total = turned if total is None else jnp.where(slot == k, turned, total)
        packed[t] = total
    for peer in range(copies.shape[0]):
        copies[peer] = block[...]


def step_body(
    start, from_one, from_two, mine, basis, wide, stress_out, velocity_out, own_sums, ends
):
    first = lanes() % 8 < 4
    for t in range(Z_PACKED):
        z_high, z_low = swapped(odd("gz"), from_one[t], from_two[t])
        both = jnp.where(first, z_low, z_high)
        for k, (f, x, yt) in enumerate(Z_TILES[16 * t : 16 * t + 16]):
            ends[f, x + DEEP, yt] = pltpu.roll(both, (124 - 8 * k) % 128, 1)

    def held(f, i, t):
        return (ends if t % 2 else wide).at[f, i, t // 2]

    top, bottom = rows() == 7, rows() == 0
    right, left = lanes() == 127, lanes() == 0

    def ring(near, far, axis, size, last, start):
        nu, fu = pltpu.roll(near, size - 1, axis), pltpu.roll(far, size - 1, axis)
        nd, fd = pltpu.roll(near, 1, axis), pltpu.roll(far, 1, axis)
        return (
            jnp.where(last, fu, nu) - jnp.where(start, fd, nd),
            jnp.where(last, nu, fu) - jnp.where(start, nd, fd),
        )

    def along_x(f, i, tiles):
        return {t: held(f, i + 1, t)[...] - held(f, i - 1, t)[...] for t in tiles}

    def along_y(f, i, tiles):
        out = {}
        for zt in (0, 1):
            if zt in tiles or zt + 2 in tiles:
                out[zt], out[zt + 2] = ring(held(f, i, zt)[...], held(f, i, zt + 2)[...], 0, 8, top, bottom)
        return out

    def along_z(f, i, tiles):
        out = {}
        for yt in (0, 2):
            if yt in tiles or yt + 1 in tiles:
                out[yt], out[yt + 1] = ring(held(f, i, yt)[...], held(f, i, yt + 1)[...], 1, 128, right, left)
        return out

    def speed(i, tiles):
        for k, (a, b, c) in enumerate(((0, 5, 4), (5, 1, 3), (4, 3, 2))):
            dx, dy, dz = along_x(a, i, tiles), along_y(b, i, tiles), along_z(c, i, tiles)
            for t in tiles:
                held(6 + k, i, t)[...] = held(6 + k, i, t)[...] + held(9, i, t)[...] * (dx[t] + dy[t] + dz[t])

    def strain(i, tiles, put):
        xx, yy, zz = along_x(6, i, tiles), along_y(7, i, tiles), along_z(8, i, tiles)
        for t in tiles:
            iso = held(10, i, t)[...] * (xx[t] + yy[t] + zz[t])
            scale = held(11, i, t)[...]
            for f, e in ((0, xx), (1, yy), (2, zz)):
                put(f, i, t, held(f, i, t)[...] + (iso + scale * e[t]))
        for f, one, other in (
            (3, along_z(7, i, tiles), along_y(8, i, tiles)),
            (4, along_z(6, i, tiles), along_x(8, i, tiles)),
            (5, along_y(6, i, tiles), along_x(7, i, tiles)),
        ):
            for t in tiles:
                put(f, i, t, held(f, i, t)[...] + 0.5 * held(11, i, t)[...] * (one[t] + other[t]))

    def keep(f, i, t, value):
        held(f, i, t)[...] = value

    def hand_out(f, i, t, value):
        stress_out[f, i - DEEP] = value

    everything = (0, 1, 2, 3)

    def loop(start, stop, body):
        def step(i, carry):
            body(i)
            return carry

        lax.fori_loop(start, stop, step, 0, unroll=2)

    def reaching(reach, body):
        for d in range(reach, 0, -1):
            tiles = tuple(t for t in everything if d + t // 2 + t % 2 <= reach)
            for i in (DEEP - d, DEEP + SIDE - 1 + d):
                body(i, tiles)
        tiles = tuple(t for t in everything if t // 2 + t % 2 <= reach)
        loop(DEEP, DEEP + SIDE, lambda i: body(i, tiles))

    reaching(3, speed)
    reaching(2, lambda i, tiles: strain(i, tiles, keep))
    reaching(1, speed)

    def last(i):
        strain(i, (0,), hand_out)
        for k in range(3):
            velocity_out[k, i - DEEP] = held(6 + k, i, 0)[...]

    loop(DEEP, DEEP + SIDE, last)

    def put(k, i, value):
        own_sums[k, pl.ds(pl.multiple_of(i * RANK, RANK), RANK), :] = value

    project(mine, odd("c"), basis, put)


def place_of(i, core):
    return (i // 2 * 2 + core) * 2 + i % 2


def project(source, core, basis, put):
    n_x, n_y, n_z = source.shape[0], source.shape[1], source.shape[2] // 3

    def cluster(i, carry):
        x, yl, half = i // 4, i // 2 % 2, i % 2
        totals = [jnp.zeros((8, 128), F32) for _ in range(3)]
        for g in range(2):
            block = source[x, (half * 2 + g) * 2 + yl]
            start = (place_of(i, core) * 2 + g) * n_z
            for z in range(n_z):
                part = basis[:, pl.ds(pl.multiple_of((start + z) * 128, 128), 128)]
                for k in range(3):
                    totals[k] = totals[k] + part * block[3 * z + k : 3 * z + k + 1, :]
        for k in range(3):
            put(k, i, totals[k])
        return carry

    lax.fori_loop(0, n_x * n_y // 2, cluster, 0)


def panels_body(other, own_sums, basis, ranks, traction, near, far, out, sums):
    def put(k, at, value):
        sums[k, pl.ds(pl.multiple_of(at * RANK, RANK), RANK), :] = value

    project(other, 1 - odd("c"), basis, lambda k, i, value: put(k, place_of(i, 1 - odd("c")), value))
    for i in range(own_sums.shape[1] // RANK):
        for k in range(3):
            put(k, place_of(i, odd("c")), own_sums[k, i * RANK : (i + 1) * RANK, :])
    last = (((1,), (1,)), ((), ()))
    ones = jnp.ones((8, 128), F32)
    rank_of = lax.broadcasted_iota(jnp.int32, (CLUST, CLUST * RANK), 1)
    cluster_of = lax.broadcasted_iota(jnp.int32, (CLUST, CLUST * RANK), 0)
    spread_out = (rank_of // RANK == cluster_of).astype(F32)
    limit = jnp.dot(
        jnp.broadcast_to(ranks[...].astype(F32), (8, CLUST)), spread_out, preferred_element_type=F32
    )
    rank = lax.broadcasted_iota(jnp.int32, (8, CLUST * RANK), 1) % RANK
    kept = rank.astype(F32) + 0.5 < limit
    row = lax.broadcasted_iota(jnp.int32, (8, CLUST * RANK), 0)
    projected = jnp.zeros((8, CLUST * RANK), F32)
    for k in range(3):
        total = lax.dot_general(ones, sums[k], last, precision=HIGHEST, preferred_element_type=F32)
        projected = jnp.where(kept & (row == k), total, projected)
    far_term = lax.dot_general(projected, far[...], last, precision=HIGHEST, preferred_element_type=F32)
    near_term = lax.dot_general(traction[0], near[...], last, precision=HIGHEST, preferred_element_type=F32)
    out[...] = near_term + far_term[0:3, :]


def both_ways(one, two, axis):
    peers = lax.axis_size(axis)
    pairs = [(i, i ^ 1) for i in range(peers)]
    others = [(i, i - 1 if i % 2 == 0 else i + 1) for i in range(1, peers - 1)]
    return lax.ppermute(one, axis, pairs), lax.ppermute(two, axis, others)


def spread(copies, axes):
    return lax.all_to_all(copies, axes, 0, 0)


def per_device(
    stress,
    velocity,
    lame_lambda,
    shear_modulus,
    buoyancy,
    yield_flags,
    panel_cell,
    panel_normal,
    near_block,
    far_rows,
    far_basis,
    block_ranks,
):
    tile = (SIDE, 128)
    zone = (SIDE,) + tile
    half = (FIELDS * SIDE // 2,) + tile
    x_message = (len(X_TILES),) + tile
    n_x, n_y, n_z = (lax.axis_size(a) for a in ("x", ("gy", "yl"), "gz"))
    traction_copies = (n_z, 3, 128)
    kept = [jax.ShapeDtypeStruct(a.shape, a.dtype) for a in (near_block, far_rows, block_ranks)]
    fields, block, one, two, near_block, far_rows, block_ranks = call(
        first_body,
        [(FIELDS,) + zone, traction_copies, half, half] + kept,
        [pltpu.HBM] * 11,
        scratch=[pltpu.VMEM(zone, F32)] * 3
        + [
            pltpu.VMEM(zone, jnp.int32),
            pltpu.VMEM((1, 128), jnp.int32),
            pltpu.VMEM((3, 128), F32),
            pltpu.SemaphoreType.DMA((11,)),
        ],
        name="first",
        vmem=FIRST,
    )(
        stress,
        velocity,
        lame_lambda,
        shear_modulus,
        buoyancy,
        yield_flags,
        panel_cell.reshape(1, 128),
        panel_normal,
        near_block,
        far_rows,
        block_ranks,
    )
    traction = block
    y_one, y_two = both_ways(one, two, "gy")
    block = spread(block, "gz")
    on_chip = pltpu.VMEM
    beside, one, two, block = call(
        widen_y_body,
        [(FIELDS,) + zone, x_message, x_message, (n_y, 3 * n_z, 128)],
        [on_chip] * 4,
        name="widen_y",
    )(fields, y_one, y_two, block)
    x_one, x_two = both_ways(one, two, GX)
    block = spread(block, ("gy", "yl"))
    wide_shape = (FIELDS, WIDE, 2) + tile
    packed, wide, block = call(
        ends_body,
        [(Z_PACKED,) + tile, wide_shape, (n_x, n_y, 3 * n_z, 128)],
        [on_chip] * 5,
        name="ends",
    )(fields, beside, x_one, x_two, block)
    z_one, z_two = both_ways(packed, packed, "gz")
    block = spread(block, "x")
    block, z_one, z_two = lax.optimization_barrier((block, z_one, z_two))
    other = lax.ppermute(block, "c", [(0, 1), (1, 0)])
    _, stress_out, velocity_out, own_sums = call(
        step_body,
        [wide_shape, stress.shape, velocity.shape, (3, CLUST // 2 * RANK, 128)],
        [on_chip] * 5,
        scratch=[pltpu.VMEM(wide_shape, F32)],
        in_place={0: 0},
        name="step",
        flops=20000000,
        vmem=8 << 20,
    )(wide, z_one, z_two, block, far_basis)
    displacement = panels(other, own_sums, far_basis, block_ranks, traction, near_block, far_rows)
    return stress_out, velocity_out, displacement


def panels(*operands):
    (out,) = call(
        panels_body,
        [(3, 128)],
        [pltpu.VMEM] * 7,
        scratch=[pltpu.VMEM((3, CLUST * RANK, 128), F32)],
        name="panels",
        flops=3000000,
        vmem=8 << 20,
    )(*operands)
    return out


def solution(mesh):
    shape = dict(mesh.shape)
    fine = jax.sharding.Mesh(
        mesh.devices.reshape(shape["gx"] // 4, 2, 2, shape["gy"], shape["gz"]), ALL
    )
    zones = P(GX, "gy", "gz")
    fields = P(None, GX, "gy", "gz")
    return jax.shard_map(
        per_device,
        mesh=fine,
        in_specs=(
            fields,
            fields,
            zones,
            zones,
            zones,
            zones,
            P(ALL),
            P(None, ALL),
            P(ALL, None),
            P(ALL, None),
            P(ALL, None),
            P(ALL, None),
        ),
        out_specs=(fields, fields, P(None, ALL)),
        check_vma=False,
    )
```

time: 102 us -> 75.3 us (0.74)
  waiting for transfers between devices: 19.4 us -> 2.78 us
  local copies, waits for them, and re-layouts: 14 us -> 3.59 us
  blocking collectives: 26.1 us -> 33 us
  starting transfers between devices: 30 us -> 24.8 us
    ppermute x6, waiting for transfers between devices: 14.7 us -> 2.02 us  [both_ways(): return (lax.ppermute(one, axis, pairs), lax.ppermute(two, axis, others))]
    unnamed x42 -> x16, local copies, waits for them, and re-layouts: 13.3 us -> 3.59 us
    all_to_all x2, blocking collectives: 26.1 us -> 33 us  [spread(): return lax.all_to_all(copies, axes, 0, 0)]
    all_to_all x1, waiting for transfers between devices: 4.73 us -> 0.76 us  [spread(): return lax.all_to_all(copies, axes, 0, 0)]
    ppermute x1, starting transfers between devices: 7.12 us -> 3.7 us  [per_device(): other = lax.ppermute(block, 'c', [(0, 1), (1, 0)])]
    all_to_all x1, starting transfers between devices: 6.12 us -> 3.46 us  [spread(): return lax.all_to_all(copies, axes, 0, 0)]
    pallas_call x6 -> x5, Pallas kernels: 10.7 us -> 9.84 us  [the longest x1 4.01 us: per_device(): call(step_body, [wide_shape, stress.shape, velocity.shape, (3, CLUST // 2...]
  transfers between devices with their start and end apart: 8 -> 8, of which waited for: 5 -> 2; matrix products, arithmetic and copies ran while one was open for 1% -> 0% of each run, Pallas kernels for 7% -> 5%
where the time goes in v3:
time: 75.3 us; the launch traced here: 74.7 us
  blocking collectives  33 us (44%)
  starting transfers between devices  24.8 us (33%)
  Pallas kernels  9.84 us (13%)
  local copies, waits for them, and re-layouts  3.59 us (5%)
  waiting for transfers between devices  2.78 us (4%)
  between operations  0.77 us (1%)
    all_to_all x2, blocking collectives, spread(): return lax.all_to_all(copies, axes, 0, 0)  33 us
    ppermute x6, starting transfers between devices, both_ways(): return (lax.ppermute(one, axis, pairs), lax.ppermute(two, axis, others))  17.6 us
    pallas_call x1, Pallas kernels, per_device(): call(step_body, [wide_shape, stress.shape, velocity.shape, (3, CLUST // 2...  4.01 us
    ppermute x1, starting transfers between devices, per_device(): other = lax.ppermute(block, 'c', [(0, 1), (1, 0)])  3.7 us
    unnamed x16, local copies, waits for them, and re-layouts  3.59 us
    all_to_all x1, starting transfers between devices, spread(): return lax.all_to_all(copies, axes, 0, 0)  3.46 us
    pallas_call x1, Pallas kernels, panels(): call(panels_body, [(3, 128)], [pltpu.VMEM] * 7, scratch=[pltpu.VMEM((3, C...  2.35 us
    pallas_call x1, Pallas kernels, per_device(): call(first_body, [(FIELDS,) + zone, traction_copies, half, half] + kept,...  2.29 us
  transfers between devices with their start and end apart: 8, of which 2 were waited for; matrix products, arithmetic and copies ran while one was open for 0% of the time, Pallas kernels for 5%

profile of v3, /device:TPU:1, one launch (start us, length us, event | category | flops | bytes accessed | tf_op | source)
XLA Modules:
  0.0 74.7 jit_solution(5430417428678360903)
XLA Ops:
  0.6 2.3 %first.1 = (f32[12,8,8,128]{3,2,1,0:T(8,128)}, f32[8,3,128]{2,1,0:T(4,128)}, f32[48,8,128]{2,1,0:T(8,128)}, f32[48,8,128]{2,1,0:T(8,128)}, f32[128,128]{1,0:T(8,...) custom-call(f32[6,8,8,128]{3,2,1,0:T(8,128)} %stress.1, f32[3,8,8,128]{3,2,1,0:T(8,128)} %velocity.1, f32[8,8,128]{2,1,0:T(8,128)} %lame.1, ...), custom_call_target="tpu_custom_call" | custom-call | flops 1000000 | bytes 1000000 | tf_op jit(solution)/shard_map/first/pallas_call | solution.py:367
  2.9 5.0 %collective-permute-start = (f32[48,8,128]{2,1,0:T(8,128)}, f32[48,8,128]{2,1,0:T(8,128)S(1)}, u32[]{:S(2)}, u32[]{:S(2)}) collective-permute-start(f32[48,8,128]{2,1,0:T(8,128)} %get-tuple-element.24), channel_id=1, source_target_pairs={{0,8},{8,0},{16,24},{24,16},{1,9},{9,1},{17,25},{25,17},{2,10},{10... | collective-permute-start | bytes 589832 | tf_op jit(solution)/shard_map/ppermute | solution.py:339
  8.0 0.7 collective-permute-start.1
  8.7 16.7 %all_to_all.15.block = f32[8,3,128]{2,1,0:T(4,128)S(1)} all-to-all(f32[8,3,128]{2,1,0:T(4,128)} %get-tuple-element.26.traction), channel_id=1, replica_groups=mesh['x'=4,'yl'=2,'c'=2,'gy'=4,'gz'=8] {'gz'}, dimensions={0} | all-to-all | bytes 24576 | tf_op jit(solution)/shard_map/all_to_all | solution.py:343
  25.3 0.0 collective-permute-done.from_one
  25.3 0.0 collective-permute-done.1.from_two
  25.3 1.0 %copy-done.1 = f32[12,8,8,128]{3,2,1,0:T(8,128)S(1)} copy-done((f32[12,8,8,128]{3,2,1,0:T(8,128)S(1)}, f32[12,8,8,128]{3,2,1,0:T(8,128)}, u32[]{:S(2)}) %copy-start.1) | copy-done | bytes 393240
  26.3 0.1 widen_y.1
  26.4 4.4 %collective-permute-start.2 = (f32[68,8,128]{2,1,0:T(8,128)S(1)}, f32[68,8,128]{2,1,0:T(8,128)S(1)}, u32[]{:S(2)}, u32[]{:S(2)}) collective-permute-start(f32[68,8,128]{2,1,0:T(8,128)S(1)} %get-tuple-element.28), channel_id=1, source_target_pairs={{0,32},{32,0},{64,96},{96,64},{128,160},{160,128},{192,224},{224,1... | collective-permute-start | bytes 835592 | tf_op jit(solution)/shard_map/ppermute | solution.py:339
  30.9 3.1 %collective-permute-start.3 = (f32[68,8,128]{2,1,0:T(8,128)S(1)}, f32[68,8,128]{2,1,0:T(8,128)S(1)}, u32[]{:S(2)}, u32[]{:S(2)}) collective-permute-start(f32[68,8,128]{2,1,0:T(8,128)S(1)} %get-tuple-element.29), channel_id=1, source_target_pairs={{32,64},{64,32},{96,128},{128,96},{160,192},{192,160},{224,256},{2... | collective-permute-start | bytes 835592 | tf_op jit(solution)/shard_map/ppermute | solution.py:339
  34.0 16.3 %all_to_all.16.block = f32[8,24,128]{2,1,0:T(8,128)S(1)} all-to-all(f32[8,24,128]{2,1,0:T(8,128)S(1)} %get-tuple-element.30), channel_id=1, replica_groups=mesh['x'=4,'yl'=2,'c'=2,'gy'=4,'gz'=8] {'gy','yl'}, dimensions={0} | all-to-all | bytes 196608 | tf_op jit(solution)/shard_map/all_to_all | solution.py:343
  50.3 0.0 collective-permute-done.2.from_one
  50.3 0.0 collective-permute-done.3.from_two
  50.3 1.1 %ends.1 = (f32[18,8,128]{2,1,0:T(8,128)S(1)}, f32[12,16,2,8,128]{4,3,2,1,0:T(8,128)S(1)}, f32[4,8,24,128]{3,2,1,0:T(8,128)}) custom-call(f32[12,8,8,128]{3,2,1,0:T(8,128)S(1)} %copy-done.1, f32[12,8,8,128]{3,2,1,0:T(8,128)S(1)} %get-tuple-element.27.beside, f32[68,8,128]{2,1,0:T(8,128)S(1)} %collective-permute-done.2.from_one, ...), custom_call_target="tpu_custom_call" | custom-call | flops 1000000 | bytes 1000000 | tf_op jit(solution)/shard_map/ends/pallas_call | solution.py:406
  51.4 1.2 %copy-done.2 = f32[12,16,2,8,128]{4,3,2,1,0:T(8,128)} copy-done((f32[12,16,2,8,128]{4,3,2,1,0:T(8,128)}, f32[12,16,2,8,128]{4,3,2,1,0:T(8,128)S(1)}, u32[]{:S(2)}) %copy-start.2) | copy-done | bytes 1572888
  52.5 3.5 %all-to-all-start.2 = ((f32[4,8,24,128]{3,2,1,0:T(8,128)}), f32[4,8,24,128]{3,2,1,0:T(8,128)S(1)}, u32[]{:S(2)}, u32[]{:S(2)}) async-start(f32[4,8,24,128]{3,2,1,0:T(8,128)} %get-tuple-element.32), calls=%async_computation.2 | async-start | bytes 786432 | tf_op jit(solution)/shard_map/all_to_all | solution.py:343
  56.0 0.7 collective-permute-start.5
  56.7 3.7 %collective-permute-start.4 = (f32[18,8,128]{2,1,0:T(8,128)S(1)}, f32[18,8,128]{2,1,0:T(8,128)S(1)}, u32[]{:S(2)}, u32[]{:S(2)}) collective-permute-start(f32[18,8,128]{2,1,0:T(8,128)S(1)} %get-tuple-element.33), channel_id=1, source_target_pairs={{0,1},{1,0},{2,3},{3,2},{4,5},{5,4},{6,7},{7,6},{8,9},{9,8},{10,11... | collective-permute-start | bytes 221192 | tf_op jit(solution)/shard_map/ppermute | solution.py:339
  60.4 0.0 collective-permute-done.5.from_two
  60.4 2.0 %collective-permute-done.4.from_one = f32[18,8,128]{2,1,0:T(8,128)S(1)} collective-permute-done((f32[18,8,128]{2,1,0:T(8,128)S(1)}, f32[18,8,128]{2,1,0:T(8,128)S(1)}, u32[]{:S(2)}, u32[]{:S(2)}) %collective-permute-start.4) | collective-permute-done | bytes 73760 | tf_op jit(solution)/shard_map/ppermute | solution.py:339
  62.4 0.8 %all-to-all-done.2.mine = f32[4,8,24,128]{3,2,1,0:T(8,128)S(1)} async-done(((f32[4,8,24,128]{3,2,1,0:T(8,128)}), f32[4,8,24,128]{3,2,1,0:T(8,128)S(1)}, u32[]{:S(2)}, u32[]{:S(2)}) %all-to-all-start.2) | async-done | bytes 393248 | tf_op jit(solution)/shard_map/all_to_all | solution.py:343
  63.2 3.7 %collective-permute-start.6 = (f32[4,8,24,128]{3,2,1,0:T(8,128)S(1)}, f32[4,8,24,128]{3,2,1,0:T(8,128)S(1)}, u32[]{:S(2)}, u32[]{:S(2)}) collective-permute-start(f32[4,8,24,128]{3,2,1,0:T(8,128)S(1)} %all-to-all-done.2.mine), channel_id=1, source_target_pairs={{0,32},{32,0},{1,33},{33,1},{2,34},{34,2},{3,35},{35,3},{4,36},{36... | collective-permute-start | bytes 1179656 | tf_op jit(solution)/shard_map/ppermute | solution.py:415
  66.9 0.0 copy-done
  66.9 0.0 copy-start.3
  66.9 1.4 %copy-done.3 = f32[12,16,2,8,128]{4,3,2,1,0:T(8,128)S(1)} copy-done((f32[12,16,2,8,128]{4,3,2,1,0:T(8,128)S(1)}, f32[12,16,2,8,128]{4,3,2,1,0:T(8,128)}, u32[]{:S(2)}) %copy-start.3) | copy-done | bytes 1572888
  68.3 4.0 %step.1 = (f32[12,16,2,8,128]{4,3,2,1,0:T(8,128)S(1)}, f32[6,8,8,128]{3,2,1,0:T(8,128)}, f32[3,8,8,128]{3,2,1,0:T(8,128)}, f32[3,128,128]{2,1,0:T(8,128)S(1)}) custom-call(f32[12,16,2,8,128]{4,3,2,1,0:T(8,128)S(1)} %copy-done.3, f32[18,8,128]{2,1,0:T(8,128)S(1)} %collective-permute-done.4.from_one, ...), custom_call_target="tpu_custom_call", output_to_operand_aliasing={{0}: (0, {})} | custom-call | flops 20000000 | bytes 20000000 | tf_op jit(solution)/shard_map/step/pallas_call | solution.py:416
  72.4 0.0 collective-permute-done.6.other
  72.4 0.0 copy-done.4
  72.4 0.0 copy-done.5
  72.4 0.0 copy-done.6
  72.4 0.0 copy-done.7
  72.4 2.4 %panels.1 = f32[3,128]{1,0:T(4,128)} custom-call(f32[4,8,24,128]{3,2,1,0:T(8,128)S(1)} %collective-permute-done.6.other, f32[3,128,128]{2,1,0:T(8,128)S(1)} %get-tuple-element.39.own_sums, f32[8,65536]{1,0:T(8,128)S(1)} %copy-done, s32[1,32]{1,0:T(1,128)S(1)} %copy-done.7, f32[8,3,128]{2,1,0:T(4,128)S(1)} %copy-done.5, f32[128,128]{1,0:T(8,128)S(1)} %copy-done.6, ...), custom_call_target="tpu_custom_call" | custom-call | flops 3000000 | bytes 3000000 | tf_op jit(solution)/shard_map/panels/pallas_call | solution.py:431
  (7 shorter events, 0.0 us)
Async XLA Ops:
  2.9 22.4 %collective-permute-start = (f32[48,8,128]{2,1,0:T(8,128)}, f32[48,8,128]{2,1,0:T(8,128)S(1)}, u32[]{:S(2)}, u32[]{:S(2)}) collective-permute-start(f32[48,8,128]{2,1,0:T(8,128)} %get-tuple-element.24), channel_id=1, source_target_pairs={{0,8},{8,0},{16,24},{24,16},{1,9},{9,1},{17,25},{25,17},{2,10},{10... | collective-permute-start | bytes 589832 | tf_op jit(solution)/shard_map/ppermute | solution.py:339
  8.0 17.4 %collective-permute-start.1 = (f32[48,8,128]{2,1,0:T(8,128)}, f32[48,8,128]{2,1,0:T(8,128)S(1)}, u32[]{:S(2)}, u32[]{:S(2)}) collective-permute-start(f32[48,8,128]{2,1,0:T(8,128)} %get-tuple-element.25), channel_id=1, source_target_pairs={{8,16},{16,8},{9,17},{17,9},{10,18},{18,10},{11,19},{19,11},{12,20... | collective-permute-start | bytes 589832 | tf_op jit(solution)/shard_map/ppermute | solution.py:339
  25.3 1.0 %copy-start.1 = (f32[12,8,8,128]{3,2,1,0:T(8,128)S(1)}, f32[12,8,8,128]{3,2,1,0:T(8,128)}, u32[]{:S(2)}) copy-start(f32[12,8,8,128]{3,2,1,0:T(8,128)} %get-tuple-element.23.fields) | copy-start | bytes 1179652
  26.3 40.6 %copy-start = (f32[8,65536]{1,0:T(8,128)S(1)}, f32[8,65536]{1,0:T(8,128)}, u32[]{:S(2)}) copy-start(f32[8,65536]{1,0:T(8,128)} %basis.3) | copy-start | bytes 6291460
  26.4 23.8 %collective-permute-start.2 = (f32[68,8,128]{2,1,0:T(8,128)S(1)}, f32[68,8,128]{2,1,0:T(8,128)S(1)}, u32[]{:S(2)}, u32[]{:S(2)}) collective-permute-start(f32[68,8,128]{2,1,0:T(8,128)S(1)} %get-tuple-element.28), channel_id=1, source_target_pairs={{0,32},{32,0},{64,96},{96,64},{128,160},{160,128},{192,224},{224,1... | collective-permute-start | bytes 835592 | tf_op jit(solution)/shard_map/ppermute | solution.py:339
  30.9 19.4 %collective-permute-start.3 = (f32[68,8,128]{2,1,0:T(8,128)S(1)}, f32[68,8,128]{2,1,0:T(8,128)S(1)}, u32[]{:S(2)}, u32[]{:S(2)}) collective-permute-start(f32[68,8,128]{2,1,0:T(8,128)S(1)} %get-tuple-element.29), channel_id=1, source_target_pairs={{32,64},{64,32},{96,128},{128,96},{160,192},{192,160},{224,256},{2... | collective-permute-start | bytes 835592 | tf_op jit(solution)/shard_map/ppermute | solution.py:339
  51.4 1.2 %copy-start.2 = (f32[12,16,2,8,128]{4,3,2,1,0:T(8,128)}, f32[12,16,2,8,128]{4,3,2,1,0:T(8,128)S(1)}, u32[]{:S(2)}) copy-start(f32[12,16,2,8,128]{4,3,2,1,0:T(8,128)S(1)} %get-tuple-element.31.start) | copy-start | bytes 4718596
  52.5 10.7 %all-to-all-start.2 = ((f32[4,8,24,128]{3,2,1,0:T(8,128)}), f32[4,8,24,128]{3,2,1,0:T(8,128)S(1)}, u32[]{:S(2)}, u32[]{:S(2)}) async-start(f32[4,8,24,128]{3,2,1,0:T(8,128)} %get-tuple-element.32), calls=%async_computation.2 | async-start | bytes 786432 | tf_op jit(solution)/shard_map/all_to_all | solution.py:343
  56.0 4.4 %collective-permute-start.5 = (f32[18,8,128]{2,1,0:T(8,128)S(1)}, f32[18,8,128]{2,1,0:T(8,128)S(1)}, u32[]{:S(2)}, u32[]{:S(2)}) collective-permute-start(f32[18,8,128]{2,1,0:T(8,128)S(1)} %get-tuple-element.33), channel_id=1, source_target_pairs={{1,2},{2,1},{3,4},{4,3},{5,6},{6,5},{9,10},{10,9},{11,12},{12,11},... | collective-permute-start | bytes 221192 | tf_op jit(solution)/shard_map/ppermute | solution.py:339
  56.7 5.8 %collective-permute-start.4 = (f32[18,8,128]{2,1,0:T(8,128)S(1)}, f32[18,8,128]{2,1,0:T(8,128)S(1)}, u32[]{:S(2)}, u32[]{:S(2)}) collective-permute-start(f32[18,8,128]{2,1,0:T(8,128)S(1)} %get-tuple-element.33), channel_id=1, source_target_pairs={{0,1},{1,0},{2,3},{3,2},{4,5},{5,4},{6,7},{7,6},{8,9},{9,8},{10,11... | collective-permute-start | bytes 221192 | tf_op jit(solution)/shard_map/ppermute | solution.py:339
  63.2 9.2 %collective-permute-start.6 = (f32[4,8,24,128]{3,2,1,0:T(8,128)S(1)}, f32[4,8,24,128]{3,2,1,0:T(8,128)S(1)}, u32[]{:S(2)}, u32[]{:S(2)}) collective-permute-start(f32[4,8,24,128]{3,2,1,0:T(8,128)S(1)} %all-to-all-done.2.mine), channel_id=1, source_target_pairs={{0,32},{32,0},{1,33},{33,1},{2,34},{34,2},{3,35},{35,3},{4,36},{36... | collective-permute-start | bytes 1179656 | tf_op jit(solution)/shard_map/ppermute | solution.py:415
  66.9 1.4 %copy-start.3 = (f32[12,16,2,8,128]{4,3,2,1,0:T(8,128)S(1)}, f32[12,16,2,8,128]{4,3,2,1,0:T(8,128)}, u32[]{:S(2)}) copy-start(f32[12,16,2,8,128]{4,3,2,1,0:T(8,128)} %copy-done.2) | copy-start | bytes 4718596
  68.3 4.0 %copy-start.4 = (f32[128,256]{1,0:T(8,128)S(1)}, f32[128,256]{1,0:T(8,128)}, u32[]{:S(2)}) copy-start(f32[128,256]{1,0:T(8,128)} %get-tuple-element.42.far) | copy-start | bytes 393220
  68.3 4.0 %copy-start.5 = (f32[8,3,128]{2,1,0:T(4,128)S(1)}, f32[8,3,128]{2,1,0:T(4,128)}, u32[]{:S(2)}) copy-start(f32[8,3,128]{2,1,0:T(4,128)} %get-tuple-element.26.traction) | copy-start | bytes 36868
  68.3 4.0 %copy-start.6 = (f32[128,128]{1,0:T(8,128)S(1)}, f32[128,128]{1,0:T(8,128)}, u32[]{:S(2)}) copy-start(f32[128,128]{1,0:T(8,128)} %get-tuple-element.41.near) | copy-start | bytes 196612
  68.3 4.0 %copy-start.7 = (s32[1,32]{1,0:T(1,128)S(1)}, s32[1,32]{1,0:T(1,128)}, u32[]{:S(2)}) copy-start(s32[1,32]{1,0:T(1,128)} %get-tuple-element.40.ranks) | copy-start | bytes 388

commit v4 on v3

--- a/solution.py
+++ b/solution.py
@@ -22,14 +22,26 @@
 DEEP = 4
 WIDE = SIDE + 2 * DEEP
 
+OF_X, OF_Y, OF_Z = (0, 5, 4), (5, 1, 3), (4, 3, 2)
+
+Y_TILES = [(f, d) for f in range(FIELDS) for d in range(1, REACH[f] + 1) if d < DEEP or f in OF_Y]
+
 X_TILES = [
-    (f, d, yt) for f in range(FIELDS) for d in range(1, REACH[f] + 1) for yt in (0, 1) if d + yt <= REACH[f]
+    (f, d, yt)
+    for f in range(FIELDS)
+    for d in range(1, REACH[f] + 1)
+    for yt in (0, 1)
+    if d + yt < DEEP and d + yt <= REACH[f] or d + yt == DEEP and f in (OF_X + OF_Y if yt else OF_X)
 ]
 X_AT = {t: i for i, t in enumerate(X_TILES)}
 
 
 def beyond(x):
     return max(-x, x - (SIDE - 1), 0)
+
+
+def known(f, x, yt):
+    return (f, beyond(x), yt) in X_AT if beyond(x) else True
 
 
 Z_TILES = [
@@ -37,7 +49,7 @@
     for f in range(FIELDS)
     for x in range(-DEEP, SIDE + DEEP)
     for yt in (0, 1)
-    if beyond(x) + yt + 1 <= REACH[f]
+    if beyond(x) + yt + 1 <= REACH[f] and known(f, x, yt)
 ]
 Z_AT = {t: i for i, t in enumerate(Z_TILES)}
 Z_PACKED = -(-len(Z_TILES) // 16)
@@ -120,30 +132,21 @@
             total = total + jnp.where(here[x], at, 0.0)
         picked.append(jnp.sum(total, axis=0, keepdims=True))
     n = [normal_in[k : k + 1, :] for k in range(3)]
-    for k, (a, b, c) in enumerate(((0, 5, 4), (5, 1, 3), (4, 3, 2))):
+    for k, (a, b, c) in enumerate(zip(OF_X, OF_Y, OF_Z)):
         value = picked[a] * n[0] + picked[b] * n[1] + picked[c] * n[2]
         for peer in range(traction.shape[0]):
             traction[peer, k : k + 1, :] = value
-    low = rows() < 4
-    for f in range(FIELDS):
-        for p in range(SIDE // 2):
-            a, b = fields[f, 2 * p], fields[f, 2 * p + 1]
-            i = f * (SIDE // 2) + p
-            down = jnp.where(low, a, pltpu.roll(b, 4, 0))
-            up = jnp.where(low, pltpu.roll(a, 4, 0), b)
-            one[i], two[i] = swapped(odd("gy"), up, down)
+    for i, (f, d) in enumerate(Y_TILES):
+        one[i], two[i] = swapped(odd("gy"), fields[f, :, SIDE - d, :], fields[f, :, d - 1, :])
     for copy in copies[8:]:
         copy.wait()
 
 
 def widen_y_body(fields, from_one, from_two, block, beside, one, two, copies):
-    low = rows() < 4
-    for f in range(FIELDS):
-        for p in range(SIDE // 2):
-            i = f * (SIDE // 2) + p
-            a, b = swapped(odd("gy"), from_one[i], from_two[i])
-            beside[f, 2 * p] = jnp.where(low, a, pltpu.roll(b, 4, 0))
-            beside[f, 2 * p + 1] = jnp.where(low, pltpu.roll(a, 4, 0), b)
+    for i, (f, d) in enumerate(Y_TILES):
+        high, low = swapped(odd("gy"), from_one[i], from_two[i])
+        beside[f, :, d - 1, :] = high
+        beside[f, :, SIDE - d, :] = low
     for i, (f, d, yt) in enumerate(X_TILES):
         source = beside if yt else fields
         one[i], two[i] = swapped(odd("c"), source[f, SIDE - d], source[f, d - 1])
@@ -165,7 +168,7 @@
     for f in range(FIELDS):
         for x in range(-DEEP, SIDE + DEEP):
             for yt in (0, 1):
-                if beyond(x) + yt <= REACH[f]:
+                if known(f, x, yt):
                     wide[f, x + DEEP, yt] = wide_tile(refs, f, x, yt)
     slot = lanes() // 8
     for t in range(Z_PACKED):
@@ -220,7 +223,7 @@
         return out
 
     def speed(i, tiles):
-        for k, (a, b, c) in enumerate(((0, 5, 4), (5, 1, 3), (4, 3, 2))):
+        for k, (a, b, c) in enumerate(zip(OF_X, OF_Y, OF_Z)):
             dx, dy, dz = along_x(a, i, tiles), along_y(b, i, tiles), along_z(c, i, tiles)
             for t in tiles:
                 held(6 + k, i, t)[...] = held(6 + k, i, t)[...] + held(9, i, t)[...] * (dx[t] + dy[t] + dz[t])
@@ -253,7 +256,7 @@
             body(i)
             return carry
 
-        lax.fori_loop(start, stop, step, 0, unroll=2)
+        lax.fori_loop(start, stop, step, 0, unroll=8)
 
     def reaching(reach, body):
         for d in range(reach, 0, -1):
@@ -301,7 +304,7 @@
             put(k, i, totals[k])
         return carry
 
-    lax.fori_loop(0, n_x * n_y // 2, cluster, 0)
+    lax.fori_loop(0, n_x * n_y // 2, cluster, 0, unroll=4)
 
 
 def panels_body(other, own_sums, basis, ranks, traction, near, far, out, sums):
@@ -359,7 +362,7 @@
 ):
     tile = (SIDE, 128)
     zone = (SIDE,) + tile
-    half = (FIELDS * SIDE // 2,) + tile
+    half = (len(Y_TILES),) + tile
     x_message = (len(X_TILES),) + tile
     n_x, n_y, n_z = (lax.axis_size(a) for a in ("x", ("gy", "yl"), "gz"))
     traction_copies = (n_z, 3, 128)

time: 75.3 us -> 74 us (0.983)
  Pallas kernels: 9.84 us -> 8.58 us
    pallas_call x1, Pallas kernels: 4.01 us -> 2.59 us  [per_device(): call(step_body, [wide_shape, stress.shape, velocity.shape, (3, CLUST // 2...]
  transfers between devices with their start and end apart: 8 -> 8, of which waited for: 2 -> 2; matrix products, arithmetic and copies ran while one was open for 0% -> 0% of each run, Pallas kernels for 5% -> 4%
where the time goes in v4:
time: 74 us; the launch traced here: 73.5 us
  blocking collectives  33.1 us (45%)
  starting transfers between devices  24.7 us (33%)
  Pallas kernels  8.58 us (12%)
  local copies, waits for them, and re-layouts  3.59 us (5%)
  waiting for transfers between devices  2.78 us (4%)
  between operations  0.78 us (1%)
    all_to_all x2, blocking collectives, spread(): return lax.all_to_all(copies, axes, 0, 0)  33.1 us
    ppermute x6, starting transfers between devices, both_ways(): return (lax.ppermute(one, axis, pairs), lax.ppermute(two, axis, others))  17.5 us
    ppermute x1, starting transfers between devices, per_device(): other = lax.ppermute(block, 'c', [(0, 1), (1, 0)])  3.7 us
    unnamed x16, local copies, waits for them, and re-layouts  3.59 us
    all_to_all x1, starting transfers between devices, spread(): return lax.all_to_all(copies, axes, 0, 0)  3.46 us
    pallas_call x1, Pallas kernels, per_device(): call(step_body, [wide_shape, stress.shape, velocity.shape, (3, CLUST // 2...  2.59 us
    pallas_call x1, Pallas kernels, per_device(): call(first_body, [(FIELDS,) + zone, traction_copies, half, half] + kept,...  2.44 us
    pallas_call x1, Pallas kernels, panels(): call(panels_body, [(3, 128)], [pltpu.VMEM] * 7, scratch=[pltpu.VMEM((3, C...  2.23 us
  transfers between devices with their start and end apart: 8, of which 2 were waited for; matrix products, arithmetic and copies ran while one was open for 0% of the time, Pallas kernels for 4%

profile of v4, /device:TPU:1, one launch (start us, length us, event | category | flops | bytes accessed | tf_op | source)
XLA Modules:
  0.0 73.5 jit_solution(10322788880355753133)
XLA Ops:
  0.6 2.4 %first.1 = (f32[12,8,8,128]{3,2,1,0:T(8,128)}, f32[8,3,128]{2,1,0:T(4,128)}, f32[37,8,128]{2,1,0:T(8,128)}, f32[37,8,128]{2,1,0:T(8,128)}, f32[128,128]{1,0:T(8,...) custom-call(f32[6,8,8,128]{3,2,1,0:T(8,128)} %stress.1, f32[3,8,8,128]{3,2,1,0:T(8,128)} %velocity.1, f32[8,8,128]{2,1,0:T(8,128)} %lame.1, ...), custom_call_target="tpu_custom_call" | custom-call | flops 1000000 | bytes 1000000 | tf_op jit(solution)/shard_map/first/pallas_call | solution.py:370
  3.1 5.0 %collective-permute-start = (f32[37,8,128]{2,1,0:T(8,128)}, f32[37,8,128]{2,1,0:T(8,128)S(1)}, u32[]{:S(2)}, u32[]{:S(2)}) collective-permute-start(f32[37,8,128]{2,1,0:T(8,128)} %get-tuple-element.24), channel_id=1, source_target_pairs={{0,8},{8,0},{16,24},{24,16},{1,9},{9,1},{17,25},{25,17},{2,10},{10... | collective-permute-start | bytes 454664 | tf_op jit(solution)/shard_map/ppermute | solution.py:342
  8.1 0.7 collective-permute-start.1
  8.8 0.0 copy-start
  8.8 16.8 %all_to_all.15.block = f32[8,3,128]{2,1,0:T(4,128)S(1)} all-to-all(f32[8,3,128]{2,1,0:T(4,128)} %get-tuple-element.26.traction), channel_id=1, replica_groups=mesh['x'=4,'yl'=2,'c'=2,'gy'=4,'gz'=8] {'gz'}, dimensions={0} | all-to-all | bytes 24576 | tf_op jit(solution)/shard_map/all_to_all | solution.py:346
  25.6 0.0 collective-permute-done.from_one
  25.6 0.0 collective-permute-done.1.from_two
  25.6 1.0 %copy-done.3 = f32[12,8,8,128]{3,2,1,0:T(8,128)S(1)} copy-done((f32[12,8,8,128]{3,2,1,0:T(8,128)S(1)}, f32[12,8,8,128]{3,2,1,0:T(8,128)}, u32[]{:S(2)}) %copy-start.3) | copy-done | bytes 393240
  26.6 0.2 widen_y.1
  26.9 4.3 %collective-permute-start.2 = (f32[64,8,128]{2,1,0:T(8,128)S(1)}, f32[64,8,128]{2,1,0:T(8,128)S(1)}, u32[]{:S(2)}, u32[]{:S(2)}) collective-permute-start(f32[64,8,128]{2,1,0:T(8,128)S(1)} %get-tuple-element.28), channel_id=1, source_target_pairs={{0,32},{32,0},{64,96},{96,64},{128,160},{160,128},{192,224},{224,1... | collective-permute-start | bytes 786440 | tf_op jit(solution)/shard_map/ppermute | solution.py:342
  31.2 3.1 %collective-permute-start.3 = (f32[64,8,128]{2,1,0:T(8,128)S(1)}, f32[64,8,128]{2,1,0:T(8,128)S(1)}, u32[]{:S(2)}, u32[]{:S(2)}) collective-permute-start(f32[64,8,128]{2,1,0:T(8,128)S(1)} %get-tuple-element.29), channel_id=1, source_target_pairs={{32,64},{64,32},{96,128},{128,96},{160,192},{192,160},{224,256},{2... | collective-permute-start | bytes 786440 | tf_op jit(solution)/shard_map/ppermute | solution.py:342
  34.3 16.3 %all_to_all.16.block = f32[8,24,128]{2,1,0:T(8,128)S(1)} all-to-all(f32[8,24,128]{2,1,0:T(8,128)S(1)} %get-tuple-element.30), channel_id=1, replica_groups=mesh['x'=4,'yl'=2,'c'=2,'gy'=4,'gz'=8] {'gy','yl'}, dimensions={0} | all-to-all | bytes 196608 | tf_op jit(solution)/shard_map/all_to_all | solution.py:346
  50.6 0.0 collective-permute-done.2.from_one
  50.6 0.0 collective-permute-done.3.from_two
  50.6 1.1 %ends.1 = (f32[18,8,128]{2,1,0:T(8,128)S(1)}, f32[12,16,2,8,128]{4,3,2,1,0:T(8,128)S(1)}, f32[4,8,24,128]{3,2,1,0:T(8,128)}) custom-call(f32[12,8,8,128]{3,2,1,0:T(8,128)S(1)} %copy-done.3, f32[12,8,8,128]{3,2,1,0:T(8,128)S(1)} %get-tuple-element.27.beside, f32[64,8,128]{2,1,0:T(8,128)S(1)} %collective-permute-done.2.from_one, ...), custom_call_target="tpu_custom_call" | custom-call | flops 1000000 | bytes 1000000 | tf_op jit(solution)/shard_map/ends/pallas_call | solution.py:409
  51.7 1.2 %copy-done.1 = f32[12,16,2,8,128]{4,3,2,1,0:T(8,128)} copy-done((f32[12,16,2,8,128]{4,3,2,1,0:T(8,128)}, f32[12,16,2,8,128]{4,3,2,1,0:T(8,128)S(1)}, u32[]{:S(2)}) %copy-start.1) | copy-done | bytes 1572888
  52.8 3.5 %all-to-all-start.2 = ((f32[4,8,24,128]{3,2,1,0:T(8,128)}), f32[4,8,24,128]{3,2,1,0:T(8,128)S(1)}, u32[]{:S(2)}, u32[]{:S(2)}) async-start(f32[4,8,24,128]{3,2,1,0:T(8,128)} %get-tuple-element.32), calls=%async_computation.2 | async-start | bytes 786432 | tf_op jit(solution)/shard_map/all_to_all | solution.py:346
  56.3 0.7 collective-permute-start.5
  57.0 3.7 %collective-permute-start.4 = (f32[18,8,128]{2,1,0:T(8,128)S(1)}, f32[18,8,128]{2,1,0:T(8,128)S(1)}, u32[]{:S(2)}, u32[]{:S(2)}) collective-permute-start(f32[18,8,128]{2,1,0:T(8,128)S(1)} %get-tuple-element.33), channel_id=1, source_target_pairs={{0,1},{1,0},{2,3},{3,2},{4,5},{5,4},{6,7},{7,6},{8,9},{9,8},{10,11... | collective-permute-start | bytes 221192 | tf_op jit(solution)/shard_map/ppermute | solution.py:342
  60.7 0.0 collective-permute-done.5.from_two
  60.7 2.0 %collective-permute-done.4.from_one = f32[18,8,128]{2,1,0:T(8,128)S(1)} collective-permute-done((f32[18,8,128]{2,1,0:T(8,128)S(1)}, f32[18,8,128]{2,1,0:T(8,128)S(1)}, u32[]{:S(2)}, u32[]{:S(2)}) %collective-permute-start.4) | collective-permute-done | bytes 73760 | tf_op jit(solution)/shard_map/ppermute | solution.py:342
  62.7 0.8 %all-to-all-done.2.mine = f32[4,8,24,128]{3,2,1,0:T(8,128)S(1)} async-done(((f32[4,8,24,128]{3,2,1,0:T(8,128)}), f32[4,8,24,128]{3,2,1,0:T(8,128)S(1)}, u32[]{:S(2)}, u32[]{:S(2)}) %all-to-all-start.2) | async-done | bytes 393248 | tf_op jit(solution)/shard_map/all_to_all | solution.py:346
  63.5 3.7 %collective-permute-start.6 = (f32[4,8,24,128]{3,2,1,0:T(8,128)S(1)}, f32[4,8,24,128]{3,2,1,0:T(8,128)S(1)}, u32[]{:S(2)}, u32[]{:S(2)}) collective-permute-start(f32[4,8,24,128]{3,2,1,0:T(8,128)S(1)} %all-to-all-done.2.mine), channel_id=1, source_target_pairs={{0,32},{32,0},{1,33},{33,1},{2,34},{34,2},{3,35},{35,3},{4,36},{36... | collective-permute-start | bytes 1179656 | tf_op jit(solution)/shard_map/ppermute | solution.py:418
  67.2 0.0 copy-done
  67.2 0.0 copy-start.2
  67.2 1.4 %copy-done.2 = f32[12,16,2,8,128]{4,3,2,1,0:T(8,128)S(1)} copy-done((f32[12,16,2,8,128]{4,3,2,1,0:T(8,128)S(1)}, f32[12,16,2,8,128]{4,3,2,1,0:T(8,128)}, u32[]{:S(2)}) %copy-start.2) | copy-done | bytes 1572888
  68.6 2.6 %step.1 = (f32[12,16,2,8,128]{4,3,2,1,0:T(8,128)S(1)}, f32[6,8,8,128]{3,2,1,0:T(8,128)}, f32[3,8,8,128]{3,2,1,0:T(8,128)}, f32[3,128,128]{2,1,0:T(8,128)S(1)}) custom-call(f32[12,16,2,8,128]{4,3,2,1,0:T(8,128)S(1)} %copy-done.2, f32[18,8,128]{2,1,0:T(8,128)S(1)} %collective-permute-done.4.from_one, ...), custom_call_target="tpu_custom_call", output_to_operand_aliasing={{0}: (0, {})} | custom-call | flops 20000000 | bytes 20000000 | tf_op jit(solution)/shard_map/step/pallas_call | solution.py:419
  71.2 0.0 collective-permute-done.6.other
  71.2 0.0 copy-done.4
  71.2 0.0 copy-done.6
  71.2 0.0 copy-done.7
  71.3 2.2 %panels.1 = f32[3,128]{1,0:T(4,128)} custom-call(f32[4,8,24,128]{3,2,1,0:T(8,128)S(1)} %collective-permute-done.6.other, f32[3,128,128]{2,1,0:T(8,128)S(1)} %get-tuple-element.39.own_sums, f32[8,65536]{1,0:T(8,128)S(1)} %copy-done, s32[1,32]{1,0:T(1,128)S(1)} %copy-done.7, f32[8,3,128]{2,1,0:T(4,128)S(1)} %copy-done.5, f32[128,128]{1,0:T(8,128)S(1)} %copy-done.6, ...), custom_call_target="tpu_custom_call" | custom-call | flops 3000000 | bytes 3000000 | tf_op jit(solution)/shard_map/panels/pallas_call | solution.py:434
  (7 shorter events, 0.0 us)
Async XLA Ops:
  3.1 22.5 %collective-permute-start = (f32[37,8,128]{2,1,0:T(8,128)}, f32[37,8,128]{2,1,0:T(8,128)S(1)}, u32[]{:S(2)}, u32[]{:S(2)}) collective-permute-start(f32[37,8,128]{2,1,0:T(8,128)} %get-tuple-element.24), channel_id=1, source_target_pairs={{0,8},{8,0},{16,24},{24,16},{1,9},{9,1},{17,25},{25,17},{2,10},{10... | collective-permute-start | bytes 454664 | tf_op jit(solution)/shard_map/ppermute | solution.py:342
  8.1 17.5 %collective-permute-start.1 = (f32[37,8,128]{2,1,0:T(8,128)}, f32[37,8,128]{2,1,0:T(8,128)S(1)}, u32[]{:S(2)}, u32[]{:S(2)}) collective-permute-start(f32[37,8,128]{2,1,0:T(8,128)} %get-tuple-element.25), channel_id=1, source_target_pairs={{8,16},{16,8},{9,17},{17,9},{10,18},{18,10},{11,19},{19,11},{12,20... | collective-permute-start | bytes 454664 | tf_op jit(solution)/shard_map/ppermute | solution.py:342
  8.8 58.4 %copy-start = (f32[8,65536]{1,0:T(8,128)S(1)}, f32[8,65536]{1,0:T(8,128)}, u32[]{:S(2)}) copy-start(f32[8,65536]{1,0:T(8,128)} %basis.3) | copy-start | bytes 6291460
  25.6 1.0 %copy-start.3 = (f32[12,8,8,128]{3,2,1,0:T(8,128)S(1)}, f32[12,8,8,128]{3,2,1,0:T(8,128)}, u32[]{:S(2)}) copy-start(f32[12,8,8,128]{3,2,1,0:T(8,128)} %get-tuple-element.23.fields) | copy-start | bytes 1179652
  26.9 23.7 %collective-permute-start.2 = (f32[64,8,128]{2,1,0:T(8,128)S(1)}, f32[64,8,128]{2,1,0:T(8,128)S(1)}, u32[]{:S(2)}, u32[]{:S(2)}) collective-permute-start(f32[64,8,128]{2,1,0:T(8,128)S(1)} %get-tuple-element.28), channel_id=1, source_target_pairs={{0,32},{32,0},{64,96},{96,64},{128,160},{160,128},{192,224},{224,1... | collective-permute-start | bytes 786440 | tf_op jit(solution)/shard_map/ppermute | solution.py:342
  31.2 19.4 %collective-permute-start.3 = (f32[64,8,128]{2,1,0:T(8,128)S(1)}, f32[64,8,128]{2,1,0:T(8,128)S(1)}, u32[]{:S(2)}, u32[]{:S(2)}) collective-permute-start(f32[64,8,128]{2,1,0:T(8,128)S(1)} %get-tuple-element.29), channel_id=1, source_target_pairs={{32,64},{64,32},{96,128},{128,96},{160,192},{192,160},{224,256},{2... | collective-permute-start | bytes 786440 | tf_op jit(solution)/shard_map/ppermute | solution.py:342
  51.7 1.2 %copy-start.1 = (f32[12,16,2,8,128]{4,3,2,1,0:T(8,128)}, f32[12,16,2,8,128]{4,3,2,1,0:T(8,128)S(1)}, u32[]{:S(2)}) copy-start(f32[12,16,2,8,128]{4,3,2,1,0:T(8,128)S(1)} %get-tuple-element.31.start) | copy-start | bytes 4718596
  52.8 10.7 %all-to-all-start.2 = ((f32[4,8,24,128]{3,2,1,0:T(8,128)}), f32[4,8,24,128]{3,2,1,0:T(8,128)S(1)}, u32[]{:S(2)}, u32[]{:S(2)}) async-start(f32[4,8,24,128]{3,2,1,0:T(8,128)} %get-tuple-element.32), calls=%async_computation.2 | async-start | bytes 786432 | tf_op jit(solution)/shard_map/all_to_all | solution.py:346
  56.3 4.4 %collective-permute-start.5 = (f32[18,8,128]{2,1,0:T(8,128)S(1)}, f32[18,8,128]{2,1,0:T(8,128)S(1)}, u32[]{:S(2)}, u32[]{:S(2)}) collective-permute-start(f32[18,8,128]{2,1,0:T(8,128)S(1)} %get-tuple-element.33), channel_id=1, source_target_pairs={{1,2},{2,1},{3,4},{4,3},{5,6},{6,5},{9,10},{10,9},{11,12},{12,11},... | collective-permute-start | bytes 221192 | tf_op jit(solution)/shard_map/ppermute | solution.py:342
  57.0 5.8 %collective-permute-start.4 = (f32[18,8,128]{2,1,0:T(8,128)S(1)}, f32[18,8,128]{2,1,0:T(8,128)S(1)}, u32[]{:S(2)}, u32[]{:S(2)}) collective-permute-start(f32[18,8,128]{2,1,0:T(8,128)S(1)} %get-tuple-element.33), channel_id=1, source_target_pairs={{0,1},{1,0},{2,3},{3,2},{4,5},{5,4},{6,7},{7,6},{8,9},{9,8},{10,11... | collective-permute-start | bytes 221192 | tf_op jit(solution)/shard_map/ppermute | solution.py:342
  63.5 7.7 %collective-permute-start.6 = (f32[4,8,24,128]{3,2,1,0:T(8,128)S(1)}, f32[4,8,24,128]{3,2,1,0:T(8,128)S(1)}, u32[]{:S(2)}, u32[]{:S(2)}) collective-permute-start(f32[4,8,24,128]{3,2,1,0:T(8,128)S(1)} %all-to-all-done.2.mine), channel_id=1, source_target_pairs={{0,32},{32,0},{1,33},{33,1},{2,34},{34,2},{3,35},{35,3},{4,36},{36... | collective-permute-start | bytes 1179656 | tf_op jit(solution)/shard_map/ppermute | solution.py:418
  67.2 1.4 %copy-start.2 = (f32[12,16,2,8,128]{4,3,2,1,0:T(8,128)S(1)}, f32[12,16,2,8,128]{4,3,2,1,0:T(8,128)}, u32[]{:S(2)}) copy-start(f32[12,16,2,8,128]{4,3,2,1,0:T(8,128)} %copy-done.1) | copy-start | bytes 4718596
  68.6 2.6 %copy-start.4 = (f32[128,256]{1,0:T(8,128)S(1)}, f32[128,256]{1,0:T(8,128)}, u32[]{:S(2)}) copy-start(f32[128,256]{1,0:T(8,128)} %get-tuple-element.42.far) | copy-start | bytes 393220
  68.6 2.6 %copy-start.5 = (f32[8,3,128]{2,1,0:T(4,128)S(1)}, f32[8,3,128]{2,1,0:T(4,128)}, u32[]{:S(2)}) copy-start(f32[8,3,128]{2,1,0:T(4,128)} %get-tuple-element.26.traction) | copy-start | bytes 36868
  68.6 2.6 %copy-start.6 = (f32[128,128]{1,0:T(8,128)S(1)}, f32[128,128]{1,0:T(8,128)}, u32[]{:S(2)}) copy-start(f32[128,128]{1,0:T(8,128)} %get-tuple-element.41.near) | copy-start | bytes 196612
  68.6 2.6 %copy-start.7 = (s32[1,32]{1,0:T(1,128)S(1)}, s32[1,32]{1,0:T(1,128)}, u32[]{:S(2)}) copy-start(s32[1,32]{1,0:T(1,128)} %get-tuple-element.40.ranks) | copy-start | bytes 388

commit v5 on v4

--- a/solution.py
+++ b/solution.py
@@ -63,13 +63,13 @@
     return lax.broadcasted_iota(jnp.int32, (8, 128), 0)
 
 
-def call(body, outs, specs, scratch=(), name=None, flops=1000000, vmem=4 << 20, in_place=None):
+def call(body, outs, specs, scratch=(), name=None, flops=1000000, vmem=4 << 20, in_place=None, away=()):
     spec = pl.BlockSpec(memory_space=pltpu.VMEM)
     return pl.pallas_call(
         body,
         out_shape=[s if hasattr(s, "dtype") else jax.ShapeDtypeStruct(s, F32) for s in outs],
         in_specs=[pl.BlockSpec(memory_space=m) for m in specs],
-        out_specs=[spec] * len(outs),
+        out_specs=[pl.BlockSpec(memory_space=pltpu.HBM) if i in away else spec for i in range(len(outs))],
         scratch_shapes=list(scratch),
         cost_estimate=pl.CostEstimate(flops=flops, bytes_accessed=flops, transcendentals=0),
         compiler_params=pltpu.CompilerParams(vmem_limit_bytes=vmem),
@@ -182,7 +182,9 @@
 
 
 def step_body(
-    start, from_one, from_two, mine, basis, wide, stress_out, velocity_out, own_sums, ends
+    start, from_one, from_two, mine, basis,
+    wide, stress_away, velocity_away, own_sums,
+    ends, stress_out, velocity_out, sems,
 ):
     first = lanes() % 8 < 4
     for t in range(Z_PACKED):
@@ -280,7 +282,15 @@
     def put(k, i, value):
         own_sums[k, pl.ds(pl.multiple_of(i * RANK, RANK), RANK), :] = value
 
+    stored = [
+        pltpu.make_async_copy(stress_out, stress_away, sems.at[0]),
+        pltpu.make_async_copy(velocity_out, velocity_away, sems.at[1]),
+    ]
+    for copy in stored:
+        copy.start()
     project(mine, odd("c"), basis, put)
+    for copy in stored:
+        copy.wait()
 
 
 def place_of(i, core):
@@ -420,8 +430,14 @@
         step_body,
         [wide_shape, stress.shape, velocity.shape, (3, CLUST // 2 * RANK, 128)],
         [on_chip] * 5,
-        scratch=[pltpu.VMEM(wide_shape, F32)],
+        scratch=[
+            pltpu.VMEM(wide_shape, F32),
+            pltpu.VMEM(stress.shape, F32),
+            pltpu.VMEM(velocity.shape, F32),
+            pltpu.SemaphoreType.DMA((2,)),
+        ],
         in_place={0: 0},
+        away=(1, 2),
         name="step",
         flops=20000000,
         vmem=8 << 20,

time: 74 us -> 73.6 us (level)
  transfers between devices with their start and end apart: 8 -> 8, of which waited for: 2 -> 2; matrix products, arithmetic and copies ran while one was open for 0% -> 0% of each run, Pallas kernels for 4% -> 3%
where the time goes in v5:
time: 73.6 us; the launch traced here: 73 us
  blocking collectives  33.1 us (45%)
  starting transfers between devices  24.7 us (34%)
  Pallas kernels  8.1 us (11%)
  local copies, waits for them, and re-layouts  3.59 us (5%)
  waiting for transfers between devices  2.78 us (4%)
  between operations  0.8 us (1%)
    all_to_all x2, blocking collectives, spread(): return lax.all_to_all(copies, axes, 0, 0)  33.1 us
    ppermute x6, starting transfers between devices, both_ways(): return (lax.ppermute(one, axis, pairs), lax.ppermute(two, axis, others))  17.5 us
    ppermute x1, starting transfers between devices, per_device(): other = lax.ppermute(block, 'c', [(0, 1), (1, 0)])  3.7 us
    unnamed x16, local copies, waits for them, and re-layouts  3.59 us
    all_to_all x1, starting transfers between devices, spread(): return lax.all_to_all(copies, axes, 0, 0)  3.46 us
    pallas_call x1, Pallas kernels, per_device(): call(first_body, [(FIELDS,) + zone, traction_copies, half, half] + kept,...  2.44 us
    pallas_call x1, Pallas kernels, panels(): call(panels_body, [(3, 128)], [pltpu.VMEM] * 7, scratch=[pltpu.VMEM((3, C...  2.23 us
    pallas_call x1, Pallas kernels, per_device(): call(step_body, [wide_shape, stress.shape, velocity.shape, (3, CLUST // 2...  2.11 us
  transfers between devices with their start and end apart: 8, of which 2 were waited for; matrix products, arithmetic and copies ran while one was open for 0% of the time, Pallas kernels for 3%

profile of v5, /device:TPU:1, one launch (start us, length us, event | category | flops | bytes accessed | tf_op | source)
XLA Modules:
  0.0 73.0 jit_solution(7297006692325777649)
XLA Ops:
  0.6 2.4 %first.1 = (f32[12,8,8,128]{3,2,1,0:T(8,128)}, f32[8,3,128]{2,1,0:T(4,128)}, f32[37,8,128]{2,1,0:T(8,128)}, f32[37,8,128]{2,1,0:T(8,128)}, f32[128,128]{1,0:T(8,...) custom-call(f32[6,8,8,128]{3,2,1,0:T(8,128)} %stress.1, f32[3,8,8,128]{3,2,1,0:T(8,128)} %velocity.1, f32[8,8,128]{2,1,0:T(8,128)} %lame.1, ...), custom_call_target="tpu_custom_call" | custom-call | flops 1000000 | bytes 1000000 | tf_op jit(solution)/shard_map/first/pallas_call | solution.py:380
  3.1 5.0 %collective-permute-start = (f32[37,8,128]{2,1,0:T(8,128)}, f32[37,8,128]{2,1,0:T(8,128)S(1)}, u32[]{:S(2)}, u32[]{:S(2)}) collective-permute-start(f32[37,8,128]{2,1,0:T(8,128)} %get-tuple-element.24), channel_id=1, source_target_pairs={{0,8},{8,0},{16,24},{24,16},{1,9},{9,1},{17,25},{25,17},{2,10},{10... | collective-permute-start | bytes 454664 | tf_op jit(solution)/shard_map/ppermute | solution.py:352
  8.1 0.7 collective-permute-start.1
  8.8 0.0 copy-start
  8.8 16.8 %all_to_all.15.block = f32[8,3,128]{2,1,0:T(4,128)S(1)} all-to-all(f32[8,3,128]{2,1,0:T(4,128)} %get-tuple-element.26.traction), channel_id=1, replica_groups=mesh['x'=4,'yl'=2,'c'=2,'gy'=4,'gz'=8] {'gz'}, dimensions={0} | all-to-all | bytes 24576 | tf_op jit(solution)/shard_map/all_to_all | solution.py:356
  25.6 0.0 collective-permute-done.from_one
  25.6 0.0 collective-permute-done.1.from_two
  25.6 1.0 %copy-done.3 = f32[12,8,8,128]{3,2,1,0:T(8,128)S(1)} copy-done((f32[12,8,8,128]{3,2,1,0:T(8,128)S(1)}, f32[12,8,8,128]{3,2,1,0:T(8,128)}, u32[]{:S(2)}) %copy-start.3) | copy-done | bytes 393240
  26.6 0.2 widen_y.1
  26.9 4.3 %collective-permute-start.2 = (f32[64,8,128]{2,1,0:T(8,128)S(1)}, f32[64,8,128]{2,1,0:T(8,128)S(1)}, u32[]{:S(2)}, u32[]{:S(2)}) collective-permute-start(f32[64,8,128]{2,1,0:T(8,128)S(1)} %get-tuple-element.28), channel_id=1, source_target_pairs={{0,32},{32,0},{64,96},{96,64},{128,160},{160,128},{192,224},{224,1... | collective-permute-start | bytes 786440 | tf_op jit(solution)/shard_map/ppermute | solution.py:352
  31.2 3.1 %collective-permute-start.3 = (f32[64,8,128]{2,1,0:T(8,128)S(1)}, f32[64,8,128]{2,1,0:T(8,128)S(1)}, u32[]{:S(2)}, u32[]{:S(2)}) collective-permute-start(f32[64,8,128]{2,1,0:T(8,128)S(1)} %get-tuple-element.29), channel_id=1, source_target_pairs={{32,64},{64,32},{96,128},{128,96},{160,192},{192,160},{224,256},{2... | collective-permute-start | bytes 786440 | tf_op jit(solution)/shard_map/ppermute | solution.py:352
  34.3 16.3 %all_to_all.16.block = f32[8,24,128]{2,1,0:T(8,128)S(1)} all-to-all(f32[8,24,128]{2,1,0:T(8,128)S(1)} %get-tuple-element.30), channel_id=1, replica_groups=mesh['x'=4,'yl'=2,'c'=2,'gy'=4,'gz'=8] {'gy','yl'}, dimensions={0} | all-to-all | bytes 196608 | tf_op jit(solution)/shard_map/all_to_all | solution.py:356
  50.6 0.0 collective-permute-done.2.from_one
  50.6 0.0 collective-permute-done.3.from_two
  50.6 1.1 %ends.1 = (f32[18,8,128]{2,1,0:T(8,128)S(1)}, f32[12,16,2,8,128]{4,3,2,1,0:T(8,128)S(1)}, f32[4,8,24,128]{3,2,1,0:T(8,128)}) custom-call(f32[12,8,8,128]{3,2,1,0:T(8,128)S(1)} %copy-done.3, f32[12,8,8,128]{3,2,1,0:T(8,128)S(1)} %get-tuple-element.27.beside, f32[64,8,128]{2,1,0:T(8,128)S(1)} %collective-permute-done.2.from_one, ...), custom_call_target="tpu_custom_call" | custom-call | flops 1000000 | bytes 1000000 | tf_op jit(solution)/shard_map/ends/pallas_call | solution.py:419
  51.7 1.2 %copy-done.1 = f32[12,16,2,8,128]{4,3,2,1,0:T(8,128)} copy-done((f32[12,16,2,8,128]{4,3,2,1,0:T(8,128)}, f32[12,16,2,8,128]{4,3,2,1,0:T(8,128)S(1)}, u32[]{:S(2)}) %copy-start.1) | copy-done | bytes 1572888
  52.8 3.5 %all-to-all-start.2 = ((f32[4,8,24,128]{3,2,1,0:T(8,128)}), f32[4,8,24,128]{3,2,1,0:T(8,128)S(1)}, u32[]{:S(2)}, u32[]{:S(2)}) async-start(f32[4,8,24,128]{3,2,1,0:T(8,128)} %get-tuple-element.32), calls=%async_computation.2 | async-start | bytes 786432 | tf_op jit(solution)/shard_map/all_to_all | solution.py:356
  56.3 0.7 collective-permute-start.5
  57.0 3.7 %collective-permute-start.4 = (f32[18,8,128]{2,1,0:T(8,128)S(1)}, f32[18,8,128]{2,1,0:T(8,128)S(1)}, u32[]{:S(2)}, u32[]{:S(2)}) collective-permute-start(f32[18,8,128]{2,1,0:T(8,128)S(1)} %get-tuple-element.33), channel_id=1, source_target_pairs={{0,1},{1,0},{2,3},{3,2},{4,5},{5,4},{6,7},{7,6},{8,9},{9,8},{10,11... | collective-permute-start | bytes 221192 | tf_op jit(solution)/shard_map/ppermute | solution.py:352
  60.7 0.0 collective-permute-done.5.from_two
  60.7 2.0 %collective-permute-done.4.from_one = f32[18,8,128]{2,1,0:T(8,128)S(1)} collective-permute-done((f32[18,8,128]{2,1,0:T(8,128)S(1)}, f32[18,8,128]{2,1,0:T(8,128)S(1)}, u32[]{:S(2)}, u32[]{:S(2)}) %collective-permute-start.4) | collective-permute-done | bytes 73760 | tf_op jit(solution)/shard_map/ppermute | solution.py:352
  62.7 0.8 %all-to-all-done.2.mine = f32[4,8,24,128]{3,2,1,0:T(8,128)S(1)} async-done(((f32[4,8,24,128]{3,2,1,0:T(8,128)}), f32[4,8,24,128]{3,2,1,0:T(8,128)S(1)}, u32[]{:S(2)}, u32[]{:S(2)}) %all-to-all-start.2) | async-done | bytes 393248 | tf_op jit(solution)/shard_map/all_to_all | solution.py:356
  63.5 3.7 %collective-permute-start.6 = (f32[4,8,24,128]{3,2,1,0:T(8,128)S(1)}, f32[4,8,24,128]{3,2,1,0:T(8,128)S(1)}, u32[]{:S(2)}, u32[]{:S(2)}) collective-permute-start(f32[4,8,24,128]{3,2,1,0:T(8,128)S(1)} %all-to-all-done.2.mine), channel_id=1, source_target_pairs={{0,32},{32,0},{1,33},{33,1},{2,34},{34,2},{3,35},{35,3},{4,36},{36... | collective-permute-start | bytes 1179656 | tf_op jit(solution)/shard_map/ppermute | solution.py:428
  67.2 0.0 copy-done
  67.2 0.0 copy-start.2
  67.2 1.4 %copy-done.2 = f32[12,16,2,8,128]{4,3,2,1,0:T(8,128)S(1)} copy-done((f32[12,16,2,8,128]{4,3,2,1,0:T(8,128)S(1)}, f32[12,16,2,8,128]{4,3,2,1,0:T(8,128)}, u32[]{:S(2)}) %copy-start.2) | copy-done | bytes 1572888
  68.6 2.1 %step.1 = (f32[12,16,2,8,128]{4,3,2,1,0:T(8,128)S(1)}, f32[6,8,8,128]{3,2,1,0:T(8,128)}, f32[3,8,8,128]{3,2,1,0:T(8,128)}, f32[3,128,128]{2,1,0:T(8,128)S(1)}) custom-call(f32[12,16,2,8,128]{4,3,2,1,0:T(8,128)S(1)} %copy-done.2, f32[18,8,128]{2,1,0:T(8,128)S(1)} %collective-permute-done.4.from_one, ...), custom_call_target="tpu_custom_call", output_to_operand_aliasing={{0}: (0, {})} | custom-call | flops 20000000 | bytes 20000000 | tf_op jit(solution)/shard_map/step/pallas_call | solution.py:429
  70.7 0.0 collective-permute-done.6.other
  70.8 0.0 copy-done.4
  70.8 0.0 copy-done.5
  70.8 0.0 copy-done.6
  70.8 2.2 %panels.1 = f32[3,128]{1,0:T(4,128)} custom-call(f32[4,8,24,128]{3,2,1,0:T(8,128)S(1)} %collective-permute-done.6.other, f32[3,128,128]{2,1,0:T(8,128)S(1)} %get-tuple-element.39.own_sums, f32[8,65536]{1,0:T(8,128)S(1)} %copy-done, s32[1,32]{1,0:T(1,128)S(1)} %copy-done.7, f32[8,3,128]{2,1,0:T(4,128)S(1)} %copy-done.5, f32[128,128]{1,0:T(8,128)S(1)} %copy-done.6, ...), custom_call_target="tpu_custom_call" | custom-call | flops 3000000 | bytes 3000000 | tf_op jit(solution)/shard_map/panels/pallas_call | solution.py:450
  (7 shorter events, 0.0 us)
Async XLA Ops:
  3.1 22.5 %collective-permute-start = (f32[37,8,128]{2,1,0:T(8,128)}, f32[37,8,128]{2,1,0:T(8,128)S(1)}, u32[]{:S(2)}, u32[]{:S(2)}) collective-permute-start(f32[37,8,128]{2,1,0:T(8,128)} %get-tuple-element.24), channel_id=1, source_target_pairs={{0,8},{8,0},{16,24},{24,16},{1,9},{9,1},{17,25},{25,17},{2,10},{10... | collective-permute-start | bytes 454664 | tf_op jit(solution)/shard_map/ppermute | solution.py:352
  8.1 17.5 %collective-permute-start.1 = (f32[37,8,128]{2,1,0:T(8,128)}, f32[37,8,128]{2,1,0:T(8,128)S(1)}, u32[]{:S(2)}, u32[]{:S(2)}) collective-permute-start(f32[37,8,128]{2,1,0:T(8,128)} %get-tuple-element.25), channel_id=1, source_target_pairs={{8,16},{16,8},{9,17},{17,9},{10,18},{18,10},{11,19},{19,11},{12,20... | collective-permute-start | bytes 454664 | tf_op jit(solution)/shard_map/ppermute | solution.py:352
  8.8 58.4 %copy-start = (f32[8,65536]{1,0:T(8,128)S(1)}, f32[8,65536]{1,0:T(8,128)}, u32[]{:S(2)}) copy-start(f32[8,65536]{1,0:T(8,128)} %basis.3) | copy-start | bytes 6291460
  25.6 1.0 %copy-start.3 = (f32[12,8,8,128]{3,2,1,0:T(8,128)S(1)}, f32[12,8,8,128]{3,2,1,0:T(8,128)}, u32[]{:S(2)}) copy-start(f32[12,8,8,128]{3,2,1,0:T(8,128)} %get-tuple-element.23.fields) | copy-start | bytes 1179652
  26.9 23.7 %collective-permute-start.2 = (f32[64,8,128]{2,1,0:T(8,128)S(1)}, f32[64,8,128]{2,1,0:T(8,128)S(1)}, u32[]{:S(2)}, u32[]{:S(2)}) collective-permute-start(f32[64,8,128]{2,1,0:T(8,128)S(1)} %get-tuple-element.28), channel_id=1, source_target_pairs={{0,32},{32,0},{64,96},{96,64},{128,160},{160,128},{192,224},{224,1... | collective-permute-start | bytes 786440 | tf_op jit(solution)/shard_map/ppermute | solution.py:352
  31.2 19.4 %collective-permute-start.3 = (f32[64,8,128]{2,1,0:T(8,128)S(1)}, f32[64,8,128]{2,1,0:T(8,128)S(1)}, u32[]{:S(2)}, u32[]{:S(2)}) collective-permute-start(f32[64,8,128]{2,1,0:T(8,128)S(1)} %get-tuple-element.29), channel_id=1, source_target_pairs={{32,64},{64,32},{96,128},{128,96},{160,192},{192,160},{224,256},{2... | collective-permute-start | bytes 786440 | tf_op jit(solution)/shard_map/ppermute | solution.py:352
  51.7 1.2 %copy-start.1 = (f32[12,16,2,8,128]{4,3,2,1,0:T(8,128)}, f32[12,16,2,8,128]{4,3,2,1,0:T(8,128)S(1)}, u32[]{:S(2)}) copy-start(f32[12,16,2,8,128]{4,3,2,1,0:T(8,128)S(1)} %get-tuple-element.31.start) | copy-start | bytes 4718596
  52.8 10.7 %all-to-all-start.2 = ((f32[4,8,24,128]{3,2,1,0:T(8,128)}), f32[4,8,24,128]{3,2,1,0:T(8,128)S(1)}, u32[]{:S(2)}, u32[]{:S(2)}) async-start(f32[4,8,24,128]{3,2,1,0:T(8,128)} %get-tuple-element.32), calls=%async_computation.2 | async-start | bytes 786432 | tf_op jit(solution)/shard_map/all_to_all | solution.py:356
  56.3 4.4 %collective-permute-start.5 = (f32[18,8,128]{2,1,0:T(8,128)S(1)}, f32[18,8,128]{2,1,0:T(8,128)S(1)}, u32[]{:S(2)}, u32[]{:S(2)}) collective-permute-start(f32[18,8,128]{2,1,0:T(8,128)S(1)} %get-tuple-element.33), channel_id=1, source_target_pairs={{1,2},{2,1},{3,4},{4,3},{5,6},{6,5},{9,10},{10,9},{11,12},{12,11},... | collective-permute-start | bytes 221192 | tf_op jit(solution)/shard_map/ppermute | solution.py:352
  57.0 5.8 %collective-permute-start.4 = (f32[18,8,128]{2,1,0:T(8,128)S(1)}, f32[18,8,128]{2,1,0:T(8,128)S(1)}, u32[]{:S(2)}, u32[]{:S(2)}) collective-permute-start(f32[18,8,128]{2,1,0:T(8,128)S(1)} %get-tuple-element.33), channel_id=1, source_target_pairs={{0,1},{1,0},{2,3},{3,2},{4,5},{5,4},{6,7},{7,6},{8,9},{9,8},{10,11... | collective-permute-start | bytes 221192 | tf_op jit(solution)/shard_map/ppermute | solution.py:352
  63.5 7.3 %collective-permute-start.6 = (f32[4,8,24,128]{3,2,1,0:T(8,128)S(1)}, f32[4,8,24,128]{3,2,1,0:T(8,128)S(1)}, u32[]{:S(2)}, u32[]{:S(2)}) collective-permute-start(f32[4,8,24,128]{3,2,1,0:T(8,128)S(1)} %all-to-all-done.2.mine), channel_id=1, source_target_pairs={{0,32},{32,0},{1,33},{33,1},{2,34},{34,2},{3,35},{35,3},{4,36},{36... | collective-permute-start | bytes 1179656 | tf_op jit(solution)/shard_map/ppermute | solution.py:428
  67.2 1.4 %copy-start.2 = (f32[12,16,2,8,128]{4,3,2,1,0:T(8,128)S(1)}, f32[12,16,2,8,128]{4,3,2,1,0:T(8,128)}, u32[]{:S(2)}) copy-start(f32[12,16,2,8,128]{4,3,2,1,0:T(8,128)} %copy-done.1) | copy-start | bytes 4718596
  68.6 2.1 %copy-start.4 = (f32[128,256]{1,0:T(8,128)S(1)}, f32[128,256]{1,0:T(8,128)}, u32[]{:S(2)}) copy-start(f32[128,256]{1,0:T(8,128)} %get-tuple-element.42.far) | copy-start | bytes 393220
  68.6 2.1 %copy-start.5 = (f32[8,3,128]{2,1,0:T(4,128)S(1)}, f32[8,3,128]{2,1,0:T(4,128)}, u32[]{:S(2)}) copy-start(f32[8,3,128]{2,1,0:T(4,128)} %get-tuple-element.26.traction) | copy-start | bytes 36868
  68.6 2.2 %copy-start.6 = (f32[128,128]{1,0:T(8,128)S(1)}, f32[128,128]{1,0:T(8,128)}, u32[]{:S(2)}) copy-start(f32[128,128]{1,0:T(8,128)} %get-tuple-element.41.near) | copy-start | bytes 196612
  68.6 2.2 %copy-start.7 = (s32[1,32]{1,0:T(1,128)S(1)}, s32[1,32]{1,0:T(1,128)}, u32[]{:S(2)}) copy-start(s32[1,32]{1,0:T(1,128)} %get-tuple-element.40.ranks) | copy-start | bytes 388
